TPU v7x, 32 devices: a whole 2x2x4 slice. The times are simulated.
32 devices in a mesh: chan: 16 (over z, x, core), rows: 2 (over y).
Axes of the slice: x: 2, y: 2, z: 4, core: 2. Of those that a mesh axis runs over, the one named last changes fastest.
Arguments:
- image: bfloat16 [768, 1, 32, 128], P('chan', None, 'rows'), may hold values from -3 to 3
- dw_kernel: float32 [768, 7, 7], P('chan'), may hold values from -13 to 13
- ln_gain: float32 [768], P('chan'), may hold values from 0.1 to 1.9
- w_in: bfloat16 [768, 3072], P(None, 'chan'), may hold values from -0.21875 to 0.21875
- w_out: bfloat16 [3072, 768], P('chan'), may hold values from -0.15625 to 0.15625
- layer_scale: float32 [768], P('chan'), may hold values from 0.3 to 1
- cotangent: bfloat16 [768, 1, 32, 128], P('chan', None, 'rows'), may hold values from -6 to 6
Outputs:
- block_out: bfloat16 [768, 1, 32, 128], P('chan', None, 'rows')
- grad_image: bfloat16 [768, 1, 32, 128], P('chan', None, 'rows')
- grad_kernel: float32 [768, 7, 7], P('chan')
- grad_gain: float32 [768], P('chan')
- grad_scale: float32 [768], P('chan')
- grad_w_in: float32 [768, 3072], P(None, 'chan')
- grad_w_out: float32 [3072, 768], P('chan')
All inputs are finite; a program needn't handle non-finite values.
Results may differ from a plain program's by a relative error of at most 0.018.
Values may be sent and summed in bfloat16 or wider, within the bound.
A program may use at most 64 MiB of HBM per device.

v0:
```python
import jax
import jax.numpy as jnp
from jax import lax
from jax.sharding import PartitionSpec as P

D = 768
KSIZE = 7


epsilon = 1e-06
inv_root_two = 0.7071067811865476
inv_root_two_pi = 0.3989422804014327


def extended(block, sides, width):
    for axis, dim in sides:
        count = lax.axis_size(axis)
        forward = [(i, i + 1) for i in range(count - 1)]
        backward = [(target, source) for source, target in forward]
        low = lax.ppermute(
            lax.slice_in_dim(block, block.shape[dim] - width, None, axis=dim), axis, forward
        )
        high = lax.ppermute(lax.slice_in_dim(block, 0, width, axis=dim), axis, backward)
        block = jnp.concatenate([low, block, high], axis=dim)
    return block


def gelu_slope(values):
    return (
        0.5 * (1.0 + lax.erf(values * inv_root_two))
        + values * jnp.exp(-0.5 * values * values) * inv_root_two_pi
    )


def forward_taps(padded, kernel, height, breadth):
    running = jnp.zeros((padded.shape[0], padded.shape[1], height, breadth), jnp.float32)
    for u in range(KSIZE):
        for v in range(KSIZE):
            running = (
                running
                + kernel[:, u, v][:, None, None, None]
                * padded[:, :, u : u + height, v : v + breadth]
            )
    return running


def transpose_taps(padded, kernel, height, breadth):
    running = jnp.zeros((padded.shape[0], padded.shape[1], height, breadth), jnp.float32)
    for u in range(KSIZE):
        for v in range(KSIZE):
            running = (
                running
                + kernel[:, u, v][:, None, None, None]
                * padded[:, :, 6 - u : 6 - u + height, 6 - v : 6 - v + breadth]
            )
    return running


def correlate_taps(padded, grad, height, breadth):
    columns = []
    for u in range(KSIZE):
        row_terms = []
        for v in range(KSIZE):
            row_terms.append(
                jnp.sum(grad * padded[:, :, u : u + height, v : v + breadth], axis=(1, 2, 3))
            )
        columns.append(jnp.stack(row_terms, axis=1))
    return jnp.stack(columns, axis=1)


def body(image, dw_kernel, ln_gain, w_in, w_out, layer_scale, cotangent):
    channels, images, height, breadth = image.shape
    pixels = images * height * breadth
    contract_lead = (((0,), (0,)), ((), ()))
    contract_tail = (((1,), (1,)), ((), ()))
    rimmed_image = extended(image, (("rows", 2),), 3)
    padded = jnp.pad(rimmed_image.astype(jnp.float32), ((0, 0), (0, 0), (0, 0), (3, 3)))
    mixed_in = forward_taps(padded, dw_kernel, height, breadth).astype(jnp.bfloat16)
    mixed_flat = mixed_in.reshape(channels, pixels).astype(jnp.float32)
    centre = lax.psum(jnp.sum(mixed_flat, axis=0), "chan") / D
    spread = lax.psum(jnp.sum(jnp.square(mixed_flat - centre), axis=0), "chan") / D
    inv_scale = lax.rsqrt(spread + epsilon)
    unit_norm = (mixed_flat - centre) * inv_scale
    normed = (unit_norm * ln_gain[:, None]).astype(jnp.bfloat16)
    weight_cut = w_in
    pre_act = lax.dot_general(
        weight_cut,
        lax.all_gather(normed, "chan", axis=0, tiled=True),
        contract_lead,
        preferred_element_type=jnp.float32,
    )
    activated = jax.nn.gelu(pre_act, approximate=False).astype(jnp.bfloat16)
    weight_cut = w_out
    branch = lax.psum_scatter(
        lax.dot_general(
            weight_cut, activated, contract_lead, preferred_element_type=jnp.float32
        ).astype(jnp.bfloat16),
        "chan",
        scatter_dimension=0,
        tiled=True,
    ).astype(jnp.float32)
    image_flat = image.reshape(channels, pixels).astype(jnp.float32)
    block_out = (
        (image_flat + layer_scale[:, None] * branch).astype(jnp.bfloat16).reshape(image.shape)
    )
    cotan_flat = cotangent.reshape(channels, pixels).astype(jnp.float32)
    scaled = (layer_scale[:, None] * cotan_flat).astype(jnp.bfloat16)
    portion = lax.all_gather(scaled, "chan", axis=0, tiled=True)
    weight_cut = w_out
    grad_run = jnp.dot(weight_cut, portion, preferred_element_type=jnp.float32)
    column_block = lax.dot_general(
        activated, portion, contract_tail, preferred_element_type=jnp.float32
    )
    grad_w_out = column_block
    grad_scale = jnp.sum(cotan_flat * branch, axis=1)
    grad_pre = (grad_run * gelu_slope(pre_act)).astype(jnp.bfloat16)
    grad_w_in = lax.dot_general(
        lax.all_gather(normed, "chan", axis=0, tiled=True),
        grad_pre,
        contract_tail,
        preferred_element_type=jnp.float32,
    )
    weight_cut = w_in
    grad_normed = lax.psum_scatter(
        jnp.dot(weight_cut, grad_pre, preferred_element_type=jnp.float32).astype(jnp.bfloat16),
        "chan",
        scatter_dimension=0,
        tiled=True,
    ).astype(jnp.float32)
    grad_gain = jnp.sum(grad_normed * unit_norm, axis=1)
    scaled_grad = grad_normed * ln_gain[:, None]
    total_one, total_two = lax.psum(
        (jnp.sum(scaled_grad, axis=0), jnp.sum(scaled_grad * unit_norm, axis=0)), "chan"
    )
    grad_mixed = (inv_scale * (scaled_grad - total_one / D - unit_norm * (total_two / D))).astype(
        jnp.bfloat16
    )
    grad_mixed = grad_mixed.reshape(channels, images, height, breadth)
    rimmed_grad = extended(grad_mixed, (("rows", 2),), 3)
    rimmed_grad = jnp.pad(rimmed_grad.astype(jnp.float32), ((0, 0), (0, 0), (0, 0), (3, 3)))
    spread_back = transpose_taps(rimmed_grad, dw_kernel, height, breadth)
    grad_image = (cotangent.astype(jnp.float32) + spread_back).astype(jnp.bfloat16)
    grad_kernel = correlate_taps(padded, grad_mixed.astype(jnp.float32), height, breadth)
    grad_w_in, grad_w_out, grad_kernel, grad_gain, grad_scale = (
        lax.psum(grad_w_in.astype(jnp.bfloat16), "rows").astype(jnp.float32),
        lax.psum(grad_w_out.astype(jnp.bfloat16), "rows").astype(jnp.float32),
        lax.psum(grad_kernel.astype(jnp.bfloat16), "rows").astype(jnp.float32),
        lax.psum(grad_gain.astype(jnp.bfloat16), "rows").astype(jnp.float32),
        lax.psum(grad_scale.astype(jnp.bfloat16), "rows").astype(jnp.float32),
    )
    return (block_out, grad_image, grad_kernel, grad_gain, grad_scale, grad_w_in, grad_w_out)


def solution(mesh):
    return jax.shard_map(
        body,
        mesh=mesh,
        in_specs=(
            P("chan", None, "rows", None),
            P("chan", None, None),
            P("chan"),
            P(None, "chan"),
            P("chan", None),
            P("chan"),
            P("chan", None, "rows", None),
        ),
        out_specs=(
            P("chan", None, "rows", None),
            P("chan", None, "rows", None),
            P("chan", None, None),
            P("chan"),
            P("chan"),
            P(None, "chan"),
            P("chan", None),
        ),
        check_vma=False,
    )
```

profile of v0, /device:TPU:0, one launch (start us, length us, event | category | flops | bytes accessed | tf_op | source)
XLA Modules:
  0.0 478.2 jit_solution(16257528177359169895)
XLA Ops:
  7.2 0.0 copy-start
  7.2 0.0 all-gather.3.cloned.1.call-start
  7.2 1.0 fusion.175
  8.2 4.9 %collective-permute-start = (bf16[48,1,3,128]{3,2,1,0:T(4,128)(2,1)S(1)}, bf16[48,1,3,128]{3,2,1,0:T(4,128)(2,1)S(1)}, u32[]{:S(2)}, u32[]{:S(2)}) collective-permute-start(bf16[48,1,3,128]{3,2,1,0:T(4,128)(2,1)S(1)} %get-tuple-element.87), channel_id=1, source_target_pairs={{0,1},{2,3},{4,5},{6,7},{8,9},{10,11},{12,13},{14,15},{16,17},{18,... | collective-permute-start | bytes 110600 | tf_op jit(solution)/shard_map/ppermute | solution.py:20
  13.1 1.3 collective-permute-start.1
  14.4 1.0 slice_bitcast_fusion.48
  15.5 1.0 slice_bitcast_fusion.47
  16.7 1.5 slice_bitcast_fusion.46
  18.3 0.8 collective-permute-done.1
  19.1 1.1 maximum_convert_fusion
  20.2 0.0 copy-start.7
  20.2 8.4 %convert_reduce_fusion = (f32[16,128]{1,0:T(8,128)S(1)}, bf16[48,1,16,128]{3,2,1,0:T(8,128)(2,1)S(1)}) fusion(f32[48]{0:T(128)} %get-tuple-element.136, f32[48]{0:T(128)} %get-tuple-element.137, f32[48]{0:T(128)S(1)} %get-tuple-element.90, f32[48,1,22,128]{3,2,1,0:T(8,128)S(1)} %maximum_convert_fusion, f32[48]{0:T(128)S(1)} %get-tuple-element.91, ...), kind=kLoop, calls=%fused_computation.340 | loop fusion | flops 9828352 | bytes 3571264 | tf_op jit(solution)/shard_map/reduce_sum | solution.py:80
  29.0 32.9 %psum.63 = f32[2048]{0:T(1024)S(1)} all-reduce(f32[2048]{0:T(1024)S(1)} %bitcast.426), channel_id=1, replica_groups=mesh['chan'=16,'rows'=2] {'chan'}, use_global_device_ids=true, to_apply=%region_1.2 | all-reduce | flops 2048 | bytes 16384 | tf_op jit(solution)/shard_map/psum | solution.py:80
  61.9 0.1 multiply_reduce_fusion
  61.9 30.0 %psum.64 = f32[2048]{0:T(1024)S(1)} all-reduce(f32[2048]{0:T(1024)S(1)} %bitcast.427), channel_id=1, replica_groups=mesh['chan'=16,'rows'=2] {'chan'}, use_global_device_ids=true, to_apply=%region_3.4 | all-reduce | flops 2048 | bytes 16384 | tf_op jit(solution)/shard_map/psum | solution.py:81
  92.0 0.8 multiply_convert_fusion
  92.8 0.0 all-gather.3.cloned.1.call-update
  92.8 0.0 copy-start.5
  92.8 0.0 reduce-scatter.7.cloned.1.call-start
  92.9 43.4 %all-gather.3.cloned.1.call-done = bf16[768,2048]{1,0:T(8,128)(2,1)} async-done(((bf16[48,2048]{1,0:T(8,128)(2,1)}), bf16[768,2048]{1,0:T(8,128)(2,1)}) %all-gather.3.cloned.1.call-update) | async-done | bytes 3145744 | tf_op jit(solution)/shard_map/all_gather | solution.py:88
  136.3 6.8 %fusion.6 = (bf16[192,2048]{1,0:T(8,128)(2,1)S(1)}, f32[192,2048]{1,0:T(8,128)}) fusion(bf16[768,192]{0,1:T(8,128)(2,1)S(1)} %copy-done, bf16[768,2048]{1,0:T(8,128)(2,1)} %all-gather.3.cloned.1.call-done), kind=kOutput, calls=%fused_computation.145 | convolution fusion | flops 629538816 | bytes 5799936 | tf_op jit(solution)/shard_map/dot_general | solution.py:86
  143.1 2.7 fusion
  145.8 4.7 copy.31
  150.5 0.0 reduce-scatter.7.cloned.1.call-update
  150.5 0.0 all-gather.5.cloned.1.call-start
  150.6 0.8 copy-done.3
  151.4 0.3 copy.22
  151.7 1.3 copy.23
  153.0 62.7 %reduce-scatter.7.cloned.1.call-done = bf16[48,2048]{1,0:T(8,128)(2,1)} async-done(((bf16[768,2048]{1,0:T(8,128)(2,1)}), bf16[48,2048]{1,0:T(8,128)(2,1)}) %reduce-scatter.7.cloned.1.call-update) | async-done | bytes 196624
  215.7 1.9 copy.32
  217.7 2.6 fusion.20
  220.3 1.9 copy.24
  222.2 0.0 all-gather.5.cloned.1.call-update
  222.2 0.0 copy-start.6
  222.2 0.2 all-reduce.7.cloned.1.call-start
  222.5 44.0 %all-gather.5.cloned.1.call-done = bf16[768,2048]{1,0:T(8,128)(2,1)} async-done(((bf16[48,2048]{1,0:T(8,128)(2,1)}), bf16[768,2048]{1,0:T(8,128)(2,1)}) %all-gather.5.cloned.1.call-update) | async-done | bytes 3145744 | tf_op jit(solution)/shard_map/all_gather | solution.py:108
  266.5 4.0 convolution_convert_fusion.2
  270.4 2.8 fusion.3
  273.2 2.0 convolution_convert_fusion.3
  275.2 0.0 all-reduce.7.cloned.1.call-update
  275.2 0.0 reduce-scatter.9.cloned.1.call-start
  275.3 2.7 fusion.1
  278.0 4.8 copy.33
  282.8 0.0 reduce-scatter.9.cloned.1.call-update
  282.8 1.0 copy-done.2
  283.8 0.9 copy.30
  284.7 19.7 %all-reduce.7.cloned.1.call-done = (bf16[768,192]{0,1:T(8,128)(2,1)}, bf16[192,768]{1,0:T(8,128)(2,1)}) async-done(((bf16[768,192]{0,1:T(8,128)(2,1)}, bf16[192,768]{1,0:T(8,128)(2,1)}), (bf16[768,192]{0,1:T(8,128)(2,1)}, bf16[192,768]{1,0:T(8,128)(2,1)})) %all-reduce.7.cloned.1.call-update) | async-done | bytes 589840 | tf_op jit(solution)/shard_map/psum | solution.py:145
  304.4 1.8 convert_element_type.162
  306.2 1.8 convert_element_type.164
  308.0 66.8 %reduce-scatter.9.cloned.1.call-done = bf16[48,2048]{1,0:T(8,128)(2,1)} async-done(((bf16[768,2048]{1,0:T(8,128)(2,1)}), bf16[48,2048]{1,0:T(8,128)(2,1)}) %reduce-scatter.9.cloned.1.call-update) | async-done | bytes 196624 | tf_op jit(solution)/shard_map/reduce_scatter | solution.py:124
  374.8 1.3 fusion.29
  376.1 57.7 %all-reduce.2 = (f32[2048]{0:T(1024)S(1)}, f32[2048]{0:T(1024)S(1)}) all-reduce(f32[2048]{0:T(1024)S(1)} %get-tuple-element.71, f32[2048]{0:T(1024)S(1)} %get-tuple-element.72), channel_id=1, replica_groups=mesh['chan'=16,'rows'=2] {'chan'}, use_global_device_ids=true, to_apply=%region_9.10 | all-reduce | flops 4096 | bytes 32768 | tf_op jit(solution)/shard_map/psum | solution.py:132
  433.8 1.1 fusion.172
  434.9 4.3 fusion.78
  439.2 4.2 fusion.77
  443.8 2.3 fusion.76
  446.2 3.4 collective-permute-start.2
  449.6 1.3 collective-permute-start.3
  451.1 9.2 %all-reduce.3 = (bf16[48,7,7]{0,2,1:T(8,128)(2,1)S(1)}, bf16[48]{0:T(256)(128)(2,1)S(1)}, bf16[48]{0:T(256)(128)(2,1)S(1)}) all-reduce(bf16[48,7,7]{0,2,1:T(8,128)(2,1)S(1)} %constant_dynamic-update-slice_fusion, bf16[48]{0:T(256)(128)(2,1)S(1)} %get-tuple-element.70, ...), channel_id=1, replica_groups=mesh['chan'=16,'rows'=2] {'rows'}, use_global_device_ids=true, to_apply=%region_59.60 | all-reduce | flops 2448 | bytes 9792 | tf_op jit(solution)/shard_map/psum | solution.py:147
  460.4 0.6 convert_element_type.156
  461.0 0.5 convert_element_type.158
  461.5 0.5 convert_element_type.160
  462.0 0.1 maximum_convert_fusion.1
  462.6 9.1 %fusion.166 = bf16[48,1,16,128]{3,2,1,0:T(8,128)(2,1)} fusion(f32[48,1,22,128]{3,2,1,0:T(8,128)S(1)} %maximum_convert_fusion.1, f32[48]{0:T(128)} %get-tuple-element.136, f32[48]{0:T(128)} %get-tuple-element.137, f32[48]{0:T(128)S(1)} %get-tuple-element.90, f32[48]{0:T(128)S(1)} %get-tuple-element.91, f32[48]{0:T(128)S(1)} %get-tuple-element.92, ...), kind=kLoop, calls=%fused_computation.320 | loop fusion | flops 9830400 | bytes 3759680 | tf_op jit(solution)/shard_map/convert_element_type | solution.py:142
  (191 shorter events, 0.8 us)
Async XLA Ops:
  7.2 129.1 %copy-start = (bf16[768,192]{0,1:T(8,128)(2,1)S(1)}, bf16[768,192]{0,1:T(8,128)(2,1)}, u32[]{:S(2)}) copy-start(bf16[768,192]{0,1:T(8,128)(2,1)} %param.10) | copy-start | bytes 884740
  7.2 129.1 %all-gather.3.cloned.1.call-start = ((), (), s32[]{:S(2)}) async-start(), calls=%async_computation.2 | async-start | bytes 3342336 | tf_op jit(solution)/shard_map/all_gather | solution.py:88
  8.2 10.0 %collective-permute-start = (bf16[48,1,3,128]{3,2,1,0:T(4,128)(2,1)S(1)}, bf16[48,1,3,128]{3,2,1,0:T(4,128)(2,1)S(1)}, u32[]{:S(2)}, u32[]{:S(2)}) collective-permute-start(bf16[48,1,3,128]{3,2,1,0:T(4,128)(2,1)S(1)} %get-tuple-element.87), channel_id=1, source_target_pairs={{0,1},{2,3},{4,5},{6,7},{8,9},{10,11},{12,13},{14,15},{16,17},{18,... | collective-permute-start | bytes 110600 | tf_op jit(solution)/shard_map/ppermute | solution.py:20
  13.1 6.0 %collective-permute-start.1 = (bf16[48,1,3,128]{3,2,1,0:T(4,128)(2,1)S(1)}, bf16[48,1,3,128]{3,2,1,0:T(4,128)(2,1)S(1)}, u32[]{:S(2)}, u32[]{:S(2)}) collective-permute-start(bf16[48,1,3,128]{3,2,1,0:T(4,128)(2,1)S(1)} %get-tuple-element.88), channel_id=1, source_target_pairs={{1,0},{3,2},{5,4},{7,6},{9,8},{11,10},{13,12},{15,14},{17,16},{19,... | collective-permute-start | bytes 110600 | tf_op jit(solution)/shard_map/ppermute | solution.py:23
  15.4 13.2 %copy-start.8 = (f32[48]{0:T(128)}, f32[48]{0:T(128)S(1)}, u32[]{:S(2)}) copy-start(f32[48]{0:T(128)S(1)} %get-tuple-element.96) | copy-start | bytes 580
  15.4 13.2 %copy-start.10 = (f32[48]{0:T(128)}, f32[48]{0:T(128)S(1)}, u32[]{:S(2)}) copy-start(f32[48]{0:T(128)S(1)} %get-tuple-element.97) | copy-start | bytes 580
  15.4 13.2 %copy-start.12 = (f32[48]{0:T(128)}, f32[48]{0:T(128)S(1)}, u32[]{:S(2)}) copy-start(f32[48]{0:T(128)S(1)} %get-tuple-element.98) | copy-start | bytes 580
  15.4 13.2 %copy-start.14 = (f32[48]{0:T(128)}, f32[48]{0:T(128)S(1)}, u32[]{:S(2)}) copy-start(f32[48]{0:T(128)S(1)} %get-tuple-element.99) | copy-start | bytes 580
  15.4 13.2 %copy-start.16 = (f32[48]{0:T(128)}, f32[48]{0:T(128)S(1)}, u32[]{:S(2)}) copy-start(f32[48]{0:T(128)S(1)} %get-tuple-element.100) | copy-start | bytes 580
  15.5 13.2 %copy-start.18 = (f32[48]{0:T(128)}, f32[48]{0:T(128)S(1)}, u32[]{:S(2)}) copy-start(f32[48]{0:T(128)S(1)} %get-tuple-element.101) | copy-start | bytes 580
  15.5 13.2 %copy-start.20 = (f32[48]{0:T(128)}, f32[48]{0:T(128)S(1)}, u32[]{:S(2)}) copy-start(f32[48]{0:T(128)S(1)} %get-tuple-element.102) | copy-start | bytes 580
  15.5 13.2 %copy-start.22 = (f32[48]{0:T(128)}, f32[48]{0:T(128)S(1)}, u32[]{:S(2)}) copy-start(f32[48]{0:T(128)S(1)} %get-tuple-element.103) | copy-start | bytes 580
  15.5 13.2 %copy-start.24 = (f32[48]{0:T(128)}, f32[48]{0:T(128)S(1)}, u32[]{:S(2)}) copy-start(f32[48]{0:T(128)S(1)} %get-tuple-element.104) | copy-start | bytes 580
  15.5 13.2 %copy-start.26 = (f32[48]{0:T(128)}, f32[48]{0:T(128)S(1)}, u32[]{:S(2)}) copy-start(f32[48]{0:T(128)S(1)} %get-tuple-element.105) | copy-start | bytes 580
  15.5 13.2 %copy-start.28 = (f32[48]{0:T(128)}, f32[48]{0:T(128)S(1)}, u32[]{:S(2)}) copy-start(f32[48]{0:T(128)S(1)} %get-tuple-element.106) | copy-start | bytes 580
  15.5 13.2 %copy-start.30 = (f32[48]{0:T(128)}, f32[48]{0:T(128)S(1)}, u32[]{:S(2)}) copy-start(f32[48]{0:T(128)S(1)} %get-tuple-element.107) | copy-start | bytes 580
  20.2 71.8 %copy-start.7 = (f32[48]{0:T(128)S(1)}, f32[48]{0:T(128)}, u32[]{:S(2)}) copy-start(f32[48]{0:T(128)} %param.9) | copy-start | bytes 580
  92.8 50.3 %copy-start.5 = (bf16[192,768]{1,0:T(8,128)(2,1)S(1)}, bf16[192,768]{1,0:T(8,128)(2,1)}, u32[]{:S(2)}) copy-start(bf16[192,768]{1,0:T(8,128)(2,1)} %param.11) | copy-start | bytes 884740
  92.8 122.9 %reduce-scatter.7.cloned.1.call-start = ((), (), s32[]{:S(2)}) async-start(), calls=%async_computation.4 | async-start | bytes 3342336
  150.5 115.9 %all-gather.5.cloned.1.call-start = ((), (), s32[]{:S(2)}) async-start(), calls=%async_computation.3 | async-start | bytes 3342336 | tf_op jit(solution)/shard_map/all_gather | solution.py:108
  222.2 48.2 %copy-start.6 = (bf16[192,768]{1,0:T(8,128)(2,1)S(1)}, bf16[192,768]{1,0:T(8,128)(2,1)}, u32[]{:S(2)}) copy-start(bf16[192,768]{1,0:T(8,128)(2,1)} %param.11) | copy-start | bytes 884740
  222.2 82.2 %all-reduce.7.cloned.1.call-start = ((), (), s32[]{:S(2)}) async-start(), calls=%async_computation.6 | async-start | bytes 1179648 | tf_op jit(solution)/shard_map/psum | solution.py:145
  275.2 99.6 %reduce-scatter.9.cloned.1.call-start = ((), (), s32[]{:S(2)}) async-start(), calls=%async_computation.5 | async-start | bytes 3342336 | tf_op jit(solution)/shard_map/reduce_scatter | solution.py:124
  443.4 18.8 %copy-start.9 = (f32[48]{0:T(128)S(1)}, f32[48]{0:T(128)}, u32[]{:S(2)}) copy-start(f32[48]{0:T(128)} %copy-done.8) | copy-start | bytes 580
  443.4 18.8 %copy-start.11 = (f32[48]{0:T(128)S(1)}, f32[48]{0:T(128)}, u32[]{:S(2)}) copy-start(f32[48]{0:T(128)} %copy-done.10) | copy-start | bytes 580
  443.4 18.8 %copy-start.13 = (f32[48]{0:T(128)S(1)}, f32[48]{0:T(128)}, u32[]{:S(2)}) copy-start(f32[48]{0:T(128)} %copy-done.12) | copy-start | bytes 580
  443.4 18.8 %copy-start.15 = (f32[48]{0:T(128)S(1)}, f32[48]{0:T(128)}, u32[]{:S(2)}) copy-start(f32[48]{0:T(128)} %copy-done.14) | copy-start | bytes 580
  443.5 18.8 %copy-start.17 = (f32[48]{0:T(128)S(1)}, f32[48]{0:T(128)}, u32[]{:S(2)}) copy-start(f32[48]{0:T(128)} %copy-done.16) | copy-start | bytes 580
  443.5 18.8 %copy-start.19 = (f32[48]{0:T(128)S(1)}, f32[48]{0:T(128)}, u32[]{:S(2)}) copy-start(f32[48]{0:T(128)} %copy-done.18) | copy-start | bytes 580
  443.5 18.8 %copy-start.21 = (f32[48]{0:T(128)S(1)}, f32[48]{0:T(128)}, u32[]{:S(2)}) copy-start(f32[48]{0:T(128)} %copy-done.20) | copy-start | bytes 580
  443.5 18.8 %copy-start.23 = (f32[48]{0:T(128)S(1)}, f32[48]{0:T(128)}, u32[]{:S(2)}) copy-start(f32[48]{0:T(128)} %copy-done.22) | copy-start | bytes 580
  443.5 18.8 %copy-start.25 = (f32[48]{0:T(128)S(1)}, f32[48]{0:T(128)}, u32[]{:S(2)}) copy-start(f32[48]{0:T(128)} %copy-done.24) | copy-start | bytes 580
  443.5 18.8 %copy-start.27 = (f32[48]{0:T(128)S(1)}, f32[48]{0:T(128)}, u32[]{:S(2)}) copy-start(f32[48]{0:T(128)} %copy-done.26) | copy-start | bytes 580
  443.5 18.8 %copy-start.29 = (f32[48]{0:T(128)S(1)}, f32[48]{0:T(128)}, u32[]{:S(2)}) copy-start(f32[48]{0:T(128)} %copy-done.28) | copy-start | bytes 580
  443.5 18.8 %copy-start.31 = (f32[48]{0:T(128)S(1)}, f32[48]{0:T(128)}, u32[]{:S(2)}) copy-start(f32[48]{0:T(128)} %copy-done.30) | copy-start | bytes 580
  443.5 18.8 %copy-start.33 = (f32[48]{0:T(128)S(1)}, f32[48]{0:T(128)}, u32[]{:S(2)}) copy-start(f32[48]{0:T(128)} %copy-done.32) | copy-start | bytes 580
  443.5 18.8 %copy-start.35 = (f32[48]{0:T(128)S(1)}, f32[48]{0:T(128)}, u32[]{:S(2)}) copy-start(f32[48]{0:T(128)} %copy-done.34) | copy-start | bytes 580
  443.6 18.8 %copy-start.37 = (f32[48]{0:T(128)S(1)}, f32[48]{0:T(128)}, u32[]{:S(2)}) copy-start(f32[48]{0:T(128)} %copy-done.36) | copy-start | bytes 580
  443.6 18.8 %copy-start.39 = (f32[48]{0:T(128)S(1)}, f32[48]{0:T(128)}, u32[]{:S(2)}) copy-start(f32[48]{0:T(128)} %copy-done.38) | copy-start | bytes 580
  443.6 18.8 %copy-start.41 = (f32[48]{0:T(128)S(1)}, f32[48]{0:T(128)}, u32[]{:S(2)}) copy-start(f32[48]{0:T(128)} %copy-done.40) | copy-start | bytes 580
  443.6 18.8 %copy-start.43 = (f32[48]{0:T(128)S(1)}, f32[48]{0:T(128)}, u32[]{:S(2)}) copy-start(f32[48]{0:T(128)} %copy-done.42) | copy-start | bytes 580
  443.6 18.8 %copy-start.45 = (f32[48]{0:T(128)S(1)}, f32[48]{0:T(128)}, u32[]{:S(2)}) copy-start(f32[48]{0:T(128)} %copy-done.44) | copy-start | bytes 580
  443.6 18.8 %copy-start.47 = (f32[48]{0:T(128)S(1)}, f32[48]{0:T(128)}, u32[]{:S(2)}) copy-start(f32[48]{0:T(128)} %copy-done.46) | copy-start | bytes 580
  443.6 18.8 %copy-start.49 = (f32[48]{0:T(128)S(1)}, f32[48]{0:T(128)}, u32[]{:S(2)}) copy-start(f32[48]{0:T(128)} %copy-done.48) | copy-start | bytes 580
  443.6 18.8 %copy-start.51 = (f32[48]{0:T(128)S(1)}, f32[48]{0:T(128)}, u32[]{:S(2)}) copy-start(f32[48]{0:T(128)} %copy-done.50) | copy-start | bytes 580
  443.6 18.8 %copy-start.53 = (f32[48]{0:T(128)S(1)}, f32[48]{0:T(128)}, u32[]{:S(2)}) copy-start(f32[48]{0:T(128)} %copy-done.52) | copy-start | bytes 580
  443.6 18.8 %copy-start.55 = (f32[48]{0:T(128)S(1)}, f32[48]{0:T(128)}, u32[]{:S(2)}) copy-start(f32[48]{0:T(128)} %copy-done.54) | copy-start | bytes 580
  443.7 18.8 %copy-start.57 = (f32[48]{0:T(128)S(1)}, f32[48]{0:T(128)}, u32[]{:S(2)}) copy-start(f32[48]{0:T(128)} %copy-done.56) | copy-start | bytes 580
  443.7 18.8 %copy-start.59 = (f32[48]{0:T(128)S(1)}, f32[48]{0:T(128)}, u32[]{:S(2)}) copy-start(f32[48]{0:T(128)} %copy-done.58) | copy-start | bytes 580
  443.7 18.8 %copy-start.61 = (f32[48]{0:T(128)S(1)}, f32[48]{0:T(128)}, u32[]{:S(2)}) copy-start(f32[48]{0:T(128)} %copy-done.60) | copy-start | bytes 580
  443.7 18.8 %copy-start.63 = (f32[48]{0:T(128)S(1)}, f32[48]{0:T(128)}, u32[]{:S(2)}) copy-start(f32[48]{0:T(128)} %copy-done.62) | copy-start | bytes 580
  443.7 18.8 %copy-start.65 = (f32[48]{0:T(128)S(1)}, f32[48]{0:T(128)}, u32[]{:S(2)}) copy-start(f32[48]{0:T(128)} %copy-done.64) | copy-start | bytes 580
  443.7 18.8 %copy-start.67 = (f32[48]{0:T(128)S(1)}, f32[48]{0:T(128)}, u32[]{:S(2)}) copy-start(f32[48]{0:T(128)} %copy-done.66) | copy-start | bytes 580
  443.7 18.8 %copy-start.69 = (f32[48]{0:T(128)S(1)}, f32[48]{0:T(128)}, u32[]{:S(2)}) copy-start(f32[48]{0:T(128)} %copy-done.68) | copy-start | bytes 580
  443.7 18.8 %copy-start.71 = (f32[48]{0:T(128)S(1)}, f32[48]{0:T(128)}, u32[]{:S(2)}) copy-start(f32[48]{0:T(128)} %copy-done.70) | copy-start | bytes 580
  443.7 18.8 %copy-start.73 = (f32[48]{0:T(128)S(1)}, f32[48]{0:T(128)}, u32[]{:S(2)}) copy-start(f32[48]{0:T(128)} %copy-done.72) | copy-start | bytes 580
  443.7 18.8 %copy-start.75 = (f32[48]{0:T(128)S(1)}, f32[48]{0:T(128)}, u32[]{:S(2)}) copy-start(f32[48]{0:T(128)} %copy-done.74) | copy-start | bytes 580
  443.8 18.8 %copy-start.77 = (f32[48]{0:T(128)S(1)}, f32[48]{0:T(128)}, u32[]{:S(2)}) copy-start(f32[48]{0:T(128)} %copy-done.76) | copy-start | bytes 580
  443.8 18.8 %copy-start.79 = (f32[48]{0:T(128)S(1)}, f32[48]{0:T(128)}, u32[]{:S(2)}) copy-start(f32[48]{0:T(128)} %copy-done.78) | copy-start | bytes 580
  443.8 18.8 %copy-start.81 = (f32[48]{0:T(128)S(1)}, f32[48]{0:T(128)}, u32[]{:S(2)}) copy-start(f32[48]{0:T(128)} %copy-done.80) | copy-start | bytes 580
  443.8 18.8 %copy-start.83 = (f32[48]{0:T(128)S(1)}, f32[48]{0:T(128)}, u32[]{:S(2)}) copy-start(f32[48]{0:T(128)} %copy-done.82) | copy-start | bytes 580
  443.8 18.8 %copy-start.85 = (f32[48]{0:T(128)S(1)}, f32[48]{0:T(128)}, u32[]{:S(2)}) copy-start(f32[48]{0:T(128)} %copy-done.84) | copy-start | bytes 580
  446.2 15.8 %collective-permute-start.2 = (bf16[48,1,3,128]{3,2,1,0:T(4,128)(2,1)S(1)}, bf16[48,1,3,128]{3,2,1,0:T(4,128)(2,1)S(1)}, u32[]{:S(2)}, u32[]{:S(2)}) collective-permute-start(bf16[48,1,3,128]{3,2,1,0:T(4,128)(2,1)S(1)} %get-tuple-element.85), channel_id=1, source_target_pairs={{0,1},{2,3},{4,5},{6,7},{8,9},{10,11},{12,13},{14,15},{16,17},{18,... | collective-permute-start | bytes 110600 | tf_op jit(solution)/shard_map/ppermute | solution.py:20
  449.6 12.4 %collective-permute-start.3 = (bf16[48,1,3,128]{3,2,1,0:T(4,128)(2,1)S(1)}, bf16[48,1,3,128]{3,2,1,0:T(4,128)(2,1)S(1)}, u32[]{:S(2)}, u32[]{:S(2)}) collective-permute-start(bf16[48,1,3,128]{3,2,1,0:T(4,128)(2,1)S(1)} %get-tuple-element.86), channel_id=1, source_target_pairs={{1,0},{3,2},{5,4},{7,6},{9,8},{11,10},{13,12},{15,14},{17,16},{19,... | collective-permute-start | bytes 110600 | tf_op jit(solution)/shard_map/ppermute | solution.py:23
  (32 other events, 326.3 us)
Sparse Core Ops, SparseCore 0:
  92.9 43.3 all-gather.2
  150.7 65.0 reduce-scatter.6
  222.3 44.0 all-gather.4
  275.3 29.0 all-reduce.6
  308.5 66.2 reduce-scatter.8
where the time goes:
time: 479 us; the launch traced here: 478 us
  waiting for transfers between devices  238 us (50%)
  blocking collectives  130 us (27%)
  other arithmetic  40.6 us (8%)
  local copies, waits for them, and re-layouts  22.8 us (5%)
  matrix products  21 us (4%)
  between operations  15.2 us (3%)
  starting transfers between devices  11.2 us (2%)
    reduce_scatter x1, waiting for transfers between devices, body(): lax.psum_scatter(jnp.dot(weight_cut, grad_pre, preferred_element_type=jnp...  66.8 us
    unnamed x6, waiting for transfers between devices  62.8 us
    psum x1, blocking collectives, body(): lax.psum((jnp.sum(scaled_grad, axis=0), jnp.sum(scaled_grad * unit_norm,...  57.7 us
    all_gather x1, waiting for transfers between devices, body(): portion = lax.all_gather(scaled, 'chan', axis=0, tiled=True)  44 us
    all_gather x1, waiting for transfers between devices, body(): lax.all_gather(normed, 'chan', axis=0, tiled=True)  43.4 us
    psum x1, blocking collectives, body(): centre = lax.psum(jnp.sum(mixed_flat, axis=0), 'chan') / D  32.9 us
    psum x1, blocking collectives, body(): lax.psum(jnp.sum(jnp.square(mixed_flat - centre), axis=0), 'chan') / D  30 us
    psum x1, waiting for transfers between devices, body(): lax.psum(grad_w_in.astype(jnp.bfloat16), 'rows').astype(jnp.float32)  19.7 us
  transfers between devices with their start and end apart: 9, of which 6 were waited for; matrix products, arithmetic and copies ran while one was open for 4% of the time, Pallas kernels for 0%

commit v1 on v0

v1 whole, which is shorter than its diff:
```python
import functools

import jax
import jax.numpy as jnp
from jax import lax
from jax.experimental import pallas as pl
from jax.experimental.pallas import tpu as pltpu
from jax.sharding import PartitionSpec as P

D = 768
KSIZE = 7


epsilon = 1e-06
inv_root_two = 0.7071067811865476
inv_root_two_pi = 0.3989422804014327


def extended(block, sides, width):
    for axis, dim in sides:
        count = lax.axis_size(axis)
        forward = [(i, i + 1) for i in range(count - 1)]
        backward = [(target, source) for source, target in forward]
        low = lax.ppermute(
            lax.slice_in_dim(block, block.shape[dim] - width, None, axis=dim), axis, forward
        )
        high = lax.ppermute(lax.slice_in_dim(block, 0, width, axis=dim), axis, backward)
        block = jnp.concatenate([low, block, high], axis=dim)
    return block


def gelu_slope(values):
    return (
        0.5 * (1.0 + lax.erf(values * inv_root_two))
        + values * jnp.exp(-0.5 * values * values) * inv_root_two_pi
    )


def forward_taps(padded, kernel, height, breadth):
    running = jnp.zeros((padded.shape[0], padded.shape[1], height, breadth), jnp.float32)
    for u in range(KSIZE):
        for v in range(KSIZE):
            running = (
                running
                + kernel[:, u, v][:, None, None, None]
                * padded[:, :, u : u + height, v : v + breadth]
            )
    return running


def transpose_taps(padded, kernel, height, breadth):
    running = jnp.zeros((padded.shape[0], padded.shape[1], height, breadth), jnp.float32)
    for u in range(KSIZE):
        for v in range(KSIZE):
            running = (
                running
                + kernel[:, u, v][:, None, None, None]
                * padded[:, :, 6 - u : 6 - u + height, 6 - v : 6 - v + breadth]
            )
    return running


def correlate_taps(padded, grad, height, breadth):
    columns = []
    for u in range(KSIZE):
        row_terms = []
        for v in range(KSIZE):
            row_terms.append(
                jnp.sum(grad * padded[:, :, u : u + height, v : v + breadth], axis=(1, 2, 3))
            )
        columns.append(jnp.stack(row_terms, axis=1))
    return jnp.stack(columns, axis=1)

GROUP = 4
MESH = pl.DeviceIdType.MESH


def greet(n, me):
    barrier = pltpu.get_barrier_semaphore()
    for k in range(1, n):
        pl.semaphore_signal(
            barrier, inc=1, device_id={"chan": lax.rem(me + k, n)}, device_id_type=MESH
        )
    pl.semaphore_wait(barrier, n - 1)


def spread_kernel(n, part, *refs):
    count = (len(refs) - 3) // 2
    sources, targets = refs[:count], refs[count : 2 * count]
    local_sem, send_sem, recv_sem = refs[2 * count :]
    me = lax.axis_index("chan")
    greet(n, me)

    def piece(ref, peer):
        if ref.shape[-1] == part * GROUP:
            return ref.at[:, pl.ds(pl.multiple_of(lax.rem(peer, GROUP) * part, part), part)]
        return ref

    copies = []
    for k in range(1, n):
        peer = lax.rem(me + k, n)
        for a in range(count):
            copy = pltpu.make_async_remote_copy(
                src_ref=piece(sources[a], peer),
                dst_ref=targets[a].at[me],
                send_sem=send_sem.at[a, k],
                recv_sem=recv_sem.at[a, k],
                device_id={"chan": peer},
                device_id_type=MESH,
            )
            copy.start()
            copies.append(copy)
    own = []
    for a in range(count):
        copy = pltpu.make_async_copy(piece(sources[a], me), targets[a].at[me], local_sem.at[a])
        copy.start()
        own.append(copy)
    for copy in own + copies:
        copy.wait()


def collect_kernel(n, part, *refs):
    count = (len(refs) - 3) // 2
    sources, targets = refs[:count], refs[count : 2 * count]
    local_sem, send_sem, recv_sem = refs[2 * count :]
    me = lax.axis_index("chan")
    plane = lax.div(me, GROUP)
    greet(n, me)
    columns = pl.ds(pl.multiple_of(lax.rem(me, GROUP) * part, part), part)

    def piece(ref, peer):
        return ref.at[peer] if len(ref.shape) == 3 else ref

    copies = []
    for k in range(1, n):
        peer = lax.rem(me + k, n)
        for a in range(count):
            copy = pltpu.make_async_remote_copy(
                src_ref=piece(sources[a], peer),
                dst_ref=targets[a].at[plane, :, columns],
                send_sem=send_sem.at[a, k],
                recv_sem=recv_sem.at[a, k],
                device_id={"chan": peer},
                device_id_type=MESH,
            )
            copy.start()
            copies.append(copy)
    own = []
    for a in range(count):
        copy = pltpu.make_async_copy(
            piece(sources[a], me), targets[a].at[plane, :, columns], local_sem.at[a]
        )
        copy.start()
        own.append(copy)
    for copy in own + copies:
        copy.wait()


def exchange(kernel, identity, arrays, shapes, n, part):
    count = len(arrays)
    size = sum(a.size * a.dtype.itemsize for a in arrays)
    return pl.pallas_call(
        functools.partial(kernel, n, part),
        out_shape=tuple(
            jax.ShapeDtypeStruct(shape, a.dtype) for shape, a in zip(shapes, arrays)
        ),
        in_specs=[pl.BlockSpec(memory_space=pl.ANY)] * count,
        out_specs=tuple([pl.BlockSpec(memory_space=pl.ANY)] * count),
        scratch_shapes=[
            pltpu.SemaphoreType.DMA((count,)),
            pltpu.SemaphoreType.DMA((count, n)),
            pltpu.SemaphoreType.DMA((count, n)),
        ],
        compiler_params=pltpu.CompilerParams(collective_id=identity, has_side_effects=True),
        cost_estimate=pl.CostEstimate(flops=0, bytes_accessed=100 * size, transcendentals=0),
    )(*arrays)


def swap(value, axis, bit):
    n = lax.axis_size(axis)
    return lax.ppermute(value, axis, [(i, i ^ bit) for i in range(n)])


def total_over(value, axis):
    bit = 1
    while bit < lax.axis_size(axis):
        near = value.astype(jnp.bfloat16)
        value = near.astype(jnp.float32) + swap(near, axis, bit).astype(jnp.float32)
        bit *= 2
    return value


def body(image, dw_kernel, ln_gain, w_in, w_out, layer_scale, cotangent):
    channels, images, height, breadth = image.shape
    pixels = images * height * breadth
    part = pixels // GROUP
    n = lax.axis_size("chan")
    planes = n // GROUP
    contract_lead = (((0,), (0,)), ((), ()))
    contract_tail = (((1,), (1,)), ((), ()))
    bf16, f32 = jnp.bfloat16, jnp.float32
    weights = jnp.stack([w_in.T, w_out])
    weights = jnp.concatenate([weights, swap(weights, "chan", 2)], axis=1)
    weights = jnp.concatenate([weights, swap(weights, "chan", 1)], axis=1)
    rimmed_image = extended(image, (("rows", 2),), 3)
    padded = jnp.pad(rimmed_image.astype(f32), ((0, 0), (0, 0), (0, 0), (3, 3)))
    mixed_in = forward_taps(padded, dw_kernel, height, breadth).astype(bf16)
    mixed_flat = mixed_in.reshape(channels, pixels)
    cotan_flat = cotangent.reshape(channels, pixels).astype(f32)
    scaled = (layer_scale[:, None] * cotan_flat).astype(bf16)
    gain_row = jnp.pad(ln_gain[None, :], ((0, 0), (0, 128 - channels)))
    mixed_all, scaled_all, gain_all = exchange(
        spread_kernel,
        0,
        (mixed_flat, scaled, gain_row),
        ((n, channels, part), (n, channels, part), (n, 1, 128)),
        n,
        part,
    )
    mixed_all = mixed_all.reshape(n * channels, part).astype(f32)
    scaled_all = scaled_all.reshape(n * channels, part)
    gain_all = gain_all[:, 0, :channels].reshape(n * channels, 1)
    centre = jnp.mean(mixed_all, axis=0)
    spread = jnp.mean(jnp.square(mixed_all - centre), axis=0)
    inv_scale = lax.rsqrt(spread + epsilon)
    unit_all = (mixed_all - centre) * inv_scale
    normed = (unit_all * gain_all).astype(bf16)
    pre_act = jnp.dot(weights[0], normed, preferred_element_type=f32)
    grad_act = jnp.dot(weights[1], scaled_all, preferred_element_type=f32)
    activated = jax.nn.gelu(pre_act, approximate=False).astype(bf16)
    grad_pre = (grad_act * gelu_slope(pre_act)).astype(bf16)
    branch_part = lax.dot_general(
        weights[1], activated, contract_lead, preferred_element_type=f32
    ).astype(bf16)
    normed_part = lax.dot_general(weights[0], grad_pre, contract_lead, preferred_element_type=f32)
    gained_part = normed_part * gain_all
    stats = jnp.stack(
        [jnp.sum(gained_part, axis=0), jnp.sum(gained_part * unit_all, axis=0), centre, inv_scale]
    )
    grad_w_in = lax.dot_general(grad_pre, normed, contract_tail, preferred_element_type=f32)
    grad_w_out = lax.dot_general(activated, scaled_all, contract_tail, preferred_element_type=f32)
    branch_all, normed_all, stats_all = exchange(
        collect_kernel,
        1,
        (
            branch_part.reshape(n, channels, part),
            normed_part.astype(bf16).reshape(n, channels, part),
            stats,
        ),
        ((planes, channels, pixels), (planes, channels, pixels), (planes, 4, pixels)),
        n,
        part,
    )
    grads = jnp.stack([grad_w_in, grad_w_out])
    for bit in (1, 2):
        half = grads.shape[1] // 2
        grads = grads[:, :half] + swap(grads[:, half:].astype(bf16), "chan", bit).astype(f32)
    grads = total_over(grads, "rows")
    branch = jnp.sum(branch_all.astype(f32), axis=0)
    grad_normed = jnp.sum(normed_all.astype(f32), axis=0)
    total_one = jnp.sum(stats_all[:, 0], axis=0)
    total_two = jnp.sum(stats_all[:, 1], axis=0)
    centre, inv_scale = stats_all[0, 2], stats_all[0, 3]
    image_flat = image.reshape(channels, pixels).astype(f32)
    block_out = (image_flat + layer_scale[:, None] * branch).astype(bf16).reshape(image.shape)
    grad_scale = jnp.sum(cotan_flat * branch, axis=1)
    unit_norm = (mixed_flat.astype(f32) - centre) * inv_scale
    grad_gain = jnp.sum(grad_normed * unit_norm, axis=1)
    scaled_grad = grad_normed * ln_gain[:, None]
    grad_mixed = (inv_scale * (scaled_grad - total_one / D - unit_norm * (total_two / D))).astype(
        bf16
    )
    grad_mixed = grad_mixed.reshape(channels, images, height, breadth)
    rimmed_grad = extended(grad_mixed, (("rows", 2),), 3)
    rimmed_grad = jnp.pad(rimmed_grad.astype(f32), ((0, 0), (0, 0), (0, 0), (3, 3)))
    spread_back = transpose_taps(rimmed_grad, dw_kernel, height, breadth)
    grad_image = (cotangent.astype(f32) + spread_back).astype(bf16)
    grad_kernel = correlate_taps(padded, grad_mixed.astype(f32), height, breadth)
    small = jnp.concatenate(
        [grad_kernel.reshape(channels, KSIZE * KSIZE), grad_gain[:, None], grad_scale[:, None]],
        axis=1,
    )
    small = total_over(small, "rows")
    grad_kernel = small[:, : KSIZE * KSIZE].reshape(channels, KSIZE, KSIZE)
    return (
        block_out,
        grad_image,
        grad_kernel,
        small[:, KSIZE * KSIZE],
        small[:, KSIZE * KSIZE + 1],
        grads[0].T,
        grads[1],
    )


def solution(mesh):
    return jax.shard_map(
        body,
        mesh=mesh,
        in_specs=(
            P("chan", None, "rows", None),
            P("chan", None, None),
            P("chan"),
            P(None, "chan"),
            P("chan", None),
            P("chan"),
            P("chan", None, "rows", None),
        ),
        out_specs=(
            P("chan", None, "rows", None),
            P("chan", None, "rows", None),
            P("chan", None, None),
            P("chan"),
            P("chan"),
            P(None, "chan"),
            P("chan", None),
        ),
        check_vma=False,
    )
```

time: 479 us -> 216 us (0.45)
  the two profiles are of different devices: /device:TPU:0 before, /device:TPU:8 now
where the time goes in v1:
time: 216 us; the launch traced here: 215 us
  Pallas kernels  80.3 us (37%)
  other arithmetic  66.7 us (31%)
  local copies, waits for them, and re-layouts  23.7 us (11%)
  starting transfers between devices  15.1 us (7%)
  waiting for transfers between devices  14.4 us (7%)
  matrix products  11.9 us (6%)
  between operations  2.81 us (1%)
    pallas_call x2, Pallas kernels, exchange(): pl.pallas_call(functools.partial(kernel, n, part), out_shape=tuple((jax.S...  80.3 us
    reduce_sum x3, other arithmetic, correlate_taps(): jnp.sum(grad * padded[:, :, u:u + height, v:v + breadth], axis=(1, 2, 3))  20.9 us
    ppermute x6, waiting for transfers between devices, swap(): return lax.ppermute(value, axis, [(i, i ^ bit) for i in range(n)])  14.4 us
    reduce_sum x1, other arithmetic, body(): grad_gain = jnp.sum(grad_normed * unit_norm, axis=1)  10.7 us
    convert_element_type x1, other arithmetic, body(): grad_image = (cotangent.astype(f32) + spread_back).astype(bf16)  9.34 us
    convert_element_type x1, other arithmetic, body(): mixed_in = forward_taps(padded, dw_kernel, height, breadth).astype(bf16)  8.72 us
    unnamed x277, local copies, waits for them, and re-layouts  8.51 us
    ppermute x6, starting transfers between devices, swap(): return lax.ppermute(value, axis, [(i, i ^ bit) for i in range(n)])  7.11 us
  transfers between devices with their start and end apart: 10, of which 3 were waited for; matrix products, arithmetic and copies ran while one was open for 25% of the time, Pallas kernels for 18%

profile of v1, /device:TPU:8, one launch (start us, length us, event | category | flops | bytes accessed | tf_op | source)
XLA Modules:
  0.0 214.8 jit_solution(10029451585824755077)
XLA Ops:
  0.7 1.0 fusion.166
  1.7 3.4 %collective-permute-start.2 = (bf16[48,1,3,128]{3,2,1,0:T(4,128)(2,1)S(1)}, bf16[48,1,3,128]{3,2,1,0:T(4,128)(2,1)S(1)}, u32[]{:S(2)}, u32[]{:S(2)}) collective-permute-start(bf16[48,1,3,128]{3,2,1,0:T(4,128)(2,1)S(1)} %get-tuple-element.81), channel_id=1, source_target_pairs={{0,1},{2,3},{4,5},{6,7},{8,9},{10,11},{12,13},{14,15},{16,17},{18,... | collective-permute-start | bytes 110600 | tf_op jit(solution)/shard_map/ppermute | solution.py:24
  5.1 1.3 collective-permute-start.3
  6.4 1.1 pad_maximum_fusion.3
  7.5 1.6 collective-permute-start
  9.1 1.0 slice_bitcast_fusion.58
  10.2 1.0 slice_bitcast_fusion.57
  11.5 1.0 bitcast_convert_fusion
  12.4 0.8 fusion.164.refs_1_
  13.2 1.5 slice_bitcast_fusion.56
  14.8 0.5 pad.12.refs_2_
  15.5 8.7 %add_convert_fusion.1 = bf16[48,1,16,128]{3,2,1,0:T(8,128)(2,1)S(1)} fusion(f32[48,1,22,128]{3,2,1,0:T(8,128)S(1)} %maximum_convert_fusion, f32[48]{0:T(128)} %get-tuple-element.134, f32[48]{0:T(128)} %get-tuple-element.135, f32[48]{0:T(128)S(1)} %get-tuple-element.88, f32[48]{0:T(128)S(1)} %get-tuple-element.89, f32[48]{0:T(128)S(1)} %get-tuple-element.90, ...), kind=kLoop, calls=%fused_computation.346 | loop fusion | flops 9633792 | bytes 3560832 | tf_op jit(solution)/shard_map/convert_element_type | solution.py:207
  24.5 0.7 copy.20
  25.3 38.3 %shard_map.126 = (bf16[16,48,512]{2,1,0:T(8,128)(2,1)}, bf16[16,48,512]{2,1,0:T(8,128)(2,1)}, f32[16,1,128]{2,1,0:T(1,128)}) custom-call(bf16[48,2048]{1,0:T(8,128)(2,1)} %bitcast.367, bf16[48,2048]{1,0:T(8,128)(2,1)} %fusion.164.refs_1_, f32[1,128]{1,0:T(1,128)} %pad.12.refs_2_), custom_call_target="tpu_custom_call" | custom-call | bytes 39372800 | tf_op jit(solution)/shard_map/pallas_call | solution.py:162
  63.6 1.1 pad_maximum_fusion.2
  64.7 0.7 mul.1255
  66.1 1.8 collective-permute-done.1
  67.9 1.4 pad_maximum_fusion.1
  69.3 3.9 %fusion.5 = (bf16[768,512]{1,0:T(8,128)(2,1)S(1)}, f32[768,512]{1,0:T(8,128)S(1)}) fusion(bf16[768,512]{1,0:T(8,128)(2,1)S(1)} %bitcast.366, bf16[2,768,768]{2,1,0:T(8,128)(2,1)S(1)} %pad_maximum_fusion.1), kind=kOutput, calls=%fused_computation.146 | convolution fusion | flops 629538816 | bytes 4325376 | tf_op jit(solution)/shard_map/dot_general | solution.py:228
  73.2 1.7 convolution_convert_fusion
  74.9 1.1 fusion.11
  76.1 2.2 %multiply_reduce_fusion.2 = (f32[512]{0:T(512)S(1)}, f32[512]{0:T(512)S(1)}, bf16[768,512]{1,0:T(8,128)(2,1)}, bf16[768,512]{1,0:T(8,128)(2,1)}) fusion(f32[768]{0:T(1024)S(1)} %copy-done.129, f32[512]{0:T(512)S(1)} %add_rsqrt_fusion, f32[512]{0:T(512)S(1)} %broadcast_multiply_fusion, bf16[16,48,512]{2,1,0:T(8,128)(2,1)S(1)} %copy-done.3, ...), kind=kOutput, calls=%fused_computation.176 | convolution fusion | flops 607910912 | bytes 4337664 | tf_op jit(solution)/shard_map/dot_general | solution.py:235
  78.2 0.6 pad_maximum_fusion.5.refs_2_
  78.8 42.0 %shard_map.127 = (bf16[4,48,2048]{2,1,0:T(8,128)(2,1)}, bf16[4,48,2048]{2,1,0:T(8,128)(2,1)}, f32[4,4,2048]{2,1,0:T(4,128)}) custom-call(bf16[16,48,512]{2,1,0:T(8,128)(2,1)} %bitcast.364, bf16[16,48,512]{2,1,0:T(8,128)(2,1)} %bitcast.365, f32[4,512]{1,0:T(4,128)} %pad_maximum_fusion.5.refs_2_), custom_call_target="tpu_custom_call" | custom-call | bytes 158105600 | tf_op jit(solution)/shard_map/pallas_call | solution.py:162
  120.9 1.1 slice_reduce_fusion.1
  121.9 0.9 fusion.167
  123.2 2.4 %convert_reduce_fusion = (f32[48,2048]{1,0:T(8,128)S(1)}, f32[48,2048]{1,0:T(8,128)}) fusion(bf16[4,48,2048]{2,1,0:T(8,128)(2,1)} %get-tuple-element.18, bf16[4,48,2048]{2,1,0:T(8,128)(2,1)} %get-tuple-element.16), kind=kLoop, calls=%fused_computation.156 | loop fusion | flops 1376256 | bytes 2359296 | tf_op jit(solution)/shard_map/reduce_sum | solution.py:260
  126.1 13.2 %fusion.70 = (bf16[48]{0:T(256)(128)(2,1)}, bf16[48]{0:T(256)(128)(2,1)}, bf16[48]{0:T(256)(128)(2,1)}, bf16[48]{0:T(256)(128)(2,1)}, bf16[48]{0:T(256)(128)(2,1...) fusion(f32[48,1,22,128]{3,2,1,0:T(8,128)S(1)} %maximum_convert_, ...), kind=kLoop, calls=%fused_computation.238 | loop fusion | flops 14154912 | bytes 3989056 | tf_op jit(solution)/shard_map/reduce_sum | solution.py:69
  139.3 3.3 %fusion.69 = (bf16[48]{0:T(256)(128)(2,1)S(1)}, bf16[48]{0:T(256)(128)(2,1)}, bf16[48]{0:T(256)(128)(2,1)}, bf16[48]{0:T(256)(128)(2,1)}, bf16[48]{0:T(256)(128)...) fusion(bf16[48,1,16,128]{3,2,1,0:T(8,128)(2,1)S(1)} %get-tuple-, ...), kind=kLoop, calls=%fused_computation.237 | loop fusion | flops 2653584 | bytes 1574112 | tf_op jit(solution)/shard_map/reduce_sum | solution.py:69
  142.6 4.4 %fusion.71 = (bf16[48]{0:T(256)(128)(2,1)}, bf16[48]{0:T(256)(128)(2,1)}, bf16[48]{0:T(256)(128)(2,1)}, bf16[48]{0:T(256)(128)(2,1)}, bf16[48]{0:T(256)(128)(2,1...) fusion(bf16[48,1,16,128]{3,2,1,0:T(8,128)(2,1)S(1)} %get-tuple-, ...), kind=kLoop, calls=%fused_computation.239 | loop fusion | flops 3636384 | bytes 1967808 | tf_op jit(solution)/shard_map/reduce_sum | solution.py:69
  147.0 0.8 convolution_bitcast_fusion
  147.8 0.7 stack.298
  148.5 0.6 constant_dynamic-update-slice_fusion.6
  149.1 2.2 %convolution_bitcast_fusion.1 = f32[1,768,768]{2,1,0:T(8,128)S(1)} fusion(bf16[768,512]{1,0:T(8,128)(2,1)} %copy-done.10, bf16[768,512]{1,0:T(8,128)(2,1)} %get-tuple-element.76), kind=kOutput, calls=%fused_computation.143 | convolution fusion | flops 603979776 | bytes 3932160 | tf_op jit(solution)/shard_map/dot_general | solution.py:240
  151.3 1.3 fusion.2
  153.1 0.7 stack.307
  153.8 0.6 constant_dynamic-update-slice_fusion.5
  154.4 0.7 stack.316
  155.1 0.6 constant_dynamic-update-slice_fusion.4
  155.7 0.7 stack.325
  156.4 0.6 constant_dynamic-update-slice_fusion.3
  157.0 0.7 stack.334
  157.7 0.6 constant_dynamic-update-slice_fusion.2
  158.3 0.7 stack.343
  159.0 0.6 constant_dynamic-update-slice_fusion.1
  159.6 1.8 copy.16
  161.4 0.7 stack.352
  162.1 0.6 constant_dynamic-update-slice_fusion
  162.7 0.7 reshape.456
  163.4 2.2 %multiply_reduce_fusion.3 = (bf16[48]{0:T(256)(128)(2,1)S(1)}, bf16[48,1,16,128]{3,2,1,0:T(8,128)(2,1)}) fusion(f32[48,1,16,128]{3,2,1,0:T(8,128)} %bitcast.362, bf16[48,1,16,128]{3,2,1,0:T(8,128)(2,1)} %param.13, f32[48]{0:T(128)} %param.12, bf16[48,1,16,128]{3,2,1,0:T(8,128)(2,1)} %param.7), kind=kLoop, calls=%fused_computation.341 | loop fusion | flops 688080 | bytes 983328 | tf_op jit(solution)/shard_map/reduce_sum | solution.py:266
  165.6 10.7 %multiply_reduce_fusion.4 = bf16[48]{0:T(256)(128)(2,1)S(1)} fusion(f32[48,1,16,128]{3,2,1,0:T(8,128)S(1)} %bitcast.353, f32[16,128]{1,0:T(8,128)} %bitcast.375, f32[16,128]{1,0:T(8,128)} %bitcast.373, f32[48]{0:T(128)} %get-tuple-element.134, f32[48]{0:T(128)} %get-tuple-element.135, f32[48]{0:T(128)} %copy-done.17, ...), kind=kLoop, calls=%fused_computation.342 | loop fusion | flops 10125264 | bytes 3761440 | tf_op jit(solution)/shard_map/reduce_sum | solution.py:268
  176.4 2.7 %collective-permute-start.6 = (bf16[48,51]{0,1:T(8,128)(2,1)S(1)}, bf16[48,51]{0,1:T(8,128)(2,1)S(1)}, u32[]{:S(2)}, u32[]{:S(2)}) collective-permute-start(bf16[48,51]{0,1:T(8,128)(2,1)S(1)} %pad_maximum_fusion.4), channel_id=1, source_target_pairs={{0,1},{1,0},{2,3},{3,2},{4,5},{5,4},{6,7},{7,6},{8,9},{9,8},{10,11... | collective-permute-start | bytes 14696 | tf_op jit(solution)/shard_map/ppermute | solution.py:181
  179.1 1.5 fusion.1
  180.6 1.4 copy-done.2
  182.1 2.5 %collective-permute-start.8 = (bf16[2,192,768]{2,1,0:T(8,128)(2,1)S(1)}, bf16[2,192,768]{2,1,0:T(8,128)(2,1)S(1)}, u32[]{:S(2)}, u32[]{:S(2)}) collective-permute-start(bf16[2,192,768]{2,1,0:T(8,128)(2,1)S(1)} %slice.1560), channel_id=1, source_target_pairs={{0,4},{2,6},{4,0},{6,2},{8,12},{10,14},{12,8},{14,10},{16,20},{18,... | collective-permute-start | bytes 1769480 | tf_op jit(solution)/shard_map/ppermute | solution.py:181
  184.6 1.9 collective-permute-start.4
  186.5 1.3 collective-permute-start.5
  187.9 0.6 reshape.457
  188.5 0.5 slice_bitcast_fusion.8
  189.4 8.4 %collective-permute-done.8 = bf16[2,192,768]{2,1,0:T(8,128)(2,1)S(1)} collective-permute-done((bf16[2,192,768]{2,1,0:T(8,128)(2,1)S(1)}, bf16[2,192,768]{2,1,0:T(8,128)(2,1)S(1)}, u32[]{:S(2)}, u32[]{:S(2)}) %collective-permute-start.8) | collective-permute-done | bytes 589856 | tf_op jit(solution)/shard_map/ppermute | solution.py:181
  197.8 1.4 fusion.20
  200.1 9.3 %fusion.159 = bf16[48,1,16,128]{3,2,1,0:T(8,128)(2,1)} fusion(f32[48,1,22,128]{3,2,1,0:T(8,128)S(1)} %maximum_convert_fusion.1, bf16[48,1,16,128]{3,2,1,0:T(8,128)(2,1)S(1)} %copy-done.6, f32[48]{0:T(128)} %get-tuple-element.134, f32[48]{0:T(128)} %get-tuple-element.135, f32[48]{0:T(128)S(1)} %copy-done.18, f32[48]{0:T(128)S(1)} %copy-done.20, ...), kind=kLoop, calls=%fused_computation.327 | loop fusion | flops 9830400 | bytes 3757440 | tf_op jit(solution)/shard_map/convert_element_type | solution.py:277
  209.4 4.2 %collective-permute-done.9 = bf16[2,192,768]{2,1,0:T(8,128)(2,1)S(1)} collective-permute-done((bf16[2,192,768]{2,1,0:T(8,128)(2,1)S(1)}, bf16[2,192,768]{2,1,0:T(8,128)(2,1)S(1)}, u32[]{:S(2)}, u32[]{:S(2)}) %collective-permute-start.9) | collective-permute-done | bytes 589856 | tf_op jit(solution)/shard_map/ppermute | solution.py:181
  213.7 1.1 slice_bitcast_fusion.6
  (292 shorter events, 2.7 us)
Async XLA Ops:
  0.6 14.7 %copy-start.7 = (bf16[48,1,16,128]{3,2,1,0:T(8,128)(2,1)S(1)}, bf16[48,1,16,128]{3,2,1,0:T(8,128)(2,1)}, u32[]{:S(2)}) copy-start(bf16[48,1,16,128]{3,2,1,0:T(8,128)(2,1)} %param.7) | copy-start | bytes 589828
  0.6 11.8 %copy-start.131 = (f32[48]{0:T(128)S(1)}, f32[48]{0:T(128)}, u32[]{:S(2)}) copy-start(f32[48]{0:T(128)} %param.12) | copy-start | bytes 580
  0.7 14.1 %copy-start.132 = (f32[48]{0:T(128)S(1)}, f32[48]{0:T(128)}, u32[]{:S(2)}) copy-start(f32[48]{0:T(128)} %param.9) | copy-start | bytes 580
  1.7 13.6 %collective-permute-start.2 = (bf16[48,1,3,128]{3,2,1,0:T(4,128)(2,1)S(1)}, bf16[48,1,3,128]{3,2,1,0:T(4,128)(2,1)S(1)}, u32[]{:S(2)}, u32[]{:S(2)}) collective-permute-start(bf16[48,1,3,128]{3,2,1,0:T(4,128)(2,1)S(1)} %get-tuple-element.81), channel_id=1, source_target_pairs={{0,1},{2,3},{4,5},{6,7},{8,9},{10,11},{12,13},{14,15},{16,17},{18,... | collective-permute-start | bytes 110600 | tf_op jit(solution)/shard_map/ppermute | solution.py:24
  5.1 10.2 %collective-permute-start.3 = (bf16[48,1,3,128]{3,2,1,0:T(4,128)(2,1)S(1)}, bf16[48,1,3,128]{3,2,1,0:T(4,128)(2,1)S(1)}, u32[]{:S(2)}, u32[]{:S(2)}) collective-permute-start(bf16[48,1,3,128]{3,2,1,0:T(4,128)(2,1)S(1)} %get-tuple-element.82), channel_id=1, source_target_pairs={{1,0},{3,2},{5,4},{7,6},{9,8},{11,10},{13,12},{15,14},{17,16},{19,... | collective-permute-start | bytes 110600 | tf_op jit(solution)/shard_map/ppermute | solution.py:27
  7.5 56.0 %collective-permute-start = (bf16[2,192,768]{2,1,0:T(8,128)(2,1)S(1)}, bf16[2,192,768]{2,1,0:T(8,128)(2,1)S(1)}, u32[]{:S(2)}, u32[]{:S(2)}) collective-permute-start(bf16[2,192,768]{2,1,0:T(8,128)(2,1)S(1)} %pad_maximum_fusion.3), channel_id=1, source_target_pairs={{0,4},{2,6},{4,0},{6,2},{8,12},{10,14},{12,8},{14,10},{16,20},{18,... | collective-permute-start | bytes 1769480 | tf_op jit(solution)/shard_map/ppermute | solution.py:181
  10.1 14.1 %copy-start.23 = (f32[48]{0:T(128)}, f32[48]{0:T(128)S(1)}, u32[]{:S(2)}) copy-start(f32[48]{0:T(128)S(1)} %get-tuple-element.91) | copy-start | bytes 580
  10.1 14.1 %copy-start.26 = (f32[48]{0:T(128)}, f32[48]{0:T(128)S(1)}, u32[]{:S(2)}) copy-start(f32[48]{0:T(128)S(1)} %get-tuple-element.92) | copy-start | bytes 580
  10.1 14.1 %copy-start.29 = (f32[48]{0:T(128)}, f32[48]{0:T(128)S(1)}, u32[]{:S(2)}) copy-start(f32[48]{0:T(128)S(1)} %get-tuple-element.93) | copy-start | bytes 580
  10.1 14.1 %copy-start.32 = (f32[48]{0:T(128)}, f32[48]{0:T(128)S(1)}, u32[]{:S(2)}) copy-start(f32[48]{0:T(128)S(1)} %get-tuple-element.94) | copy-start | bytes 580
  10.1 14.1 %copy-start.35 = (f32[48]{0:T(128)}, f32[48]{0:T(128)S(1)}, u32[]{:S(2)}) copy-start(f32[48]{0:T(128)S(1)} %get-tuple-element.95) | copy-start | bytes 580
  10.1 14.1 %copy-start.38 = (f32[48]{0:T(128)}, f32[48]{0:T(128)S(1)}, u32[]{:S(2)}) copy-start(f32[48]{0:T(128)S(1)} %get-tuple-element.96) | copy-start | bytes 580
  10.1 14.1 %copy-start.41 = (f32[48]{0:T(128)}, f32[48]{0:T(128)S(1)}, u32[]{:S(2)}) copy-start(f32[48]{0:T(128)S(1)} %get-tuple-element.97) | copy-start | bytes 580
  10.1 14.1 %copy-start.44 = (f32[48]{0:T(128)}, f32[48]{0:T(128)S(1)}, u32[]{:S(2)}) copy-start(f32[48]{0:T(128)S(1)} %get-tuple-element.98) | copy-start | bytes 580
  10.1 14.1 %copy-start.47 = (f32[48]{0:T(128)}, f32[48]{0:T(128)S(1)}, u32[]{:S(2)}) copy-start(f32[48]{0:T(128)S(1)} %get-tuple-element.99) | copy-start | bytes 580
  10.2 14.1 %copy-start.50 = (f32[48]{0:T(128)}, f32[48]{0:T(128)S(1)}, u32[]{:S(2)}) copy-start(f32[48]{0:T(128)S(1)} %get-tuple-element.100) | copy-start | bytes 580
  10.2 14.1 %copy-start.53 = (f32[48]{0:T(128)}, f32[48]{0:T(128)S(1)}, u32[]{:S(2)}) copy-start(f32[48]{0:T(128)S(1)} %get-tuple-element.101) | copy-start | bytes 580
  10.2 14.1 %copy-start.56 = (f32[48]{0:T(128)}, f32[48]{0:T(128)S(1)}, u32[]{:S(2)}) copy-start(f32[48]{0:T(128)S(1)} %get-tuple-element.102) | copy-start | bytes 580
  10.2 14.1 %copy-start.59 = (f32[48]{0:T(128)}, f32[48]{0:T(128)S(1)}, u32[]{:S(2)}) copy-start(f32[48]{0:T(128)S(1)} %get-tuple-element.103) | copy-start | bytes 580
  10.2 14.1 %copy-start.62 = (f32[48]{0:T(128)}, f32[48]{0:T(128)S(1)}, u32[]{:S(2)}) copy-start(f32[48]{0:T(128)S(1)} %get-tuple-element.104) | copy-start | bytes 580
  10.2 14.1 %copy-start.65 = (f32[48]{0:T(128)}, f32[48]{0:T(128)S(1)}, u32[]{:S(2)}) copy-start(f32[48]{0:T(128)S(1)} %get-tuple-element.105) | copy-start | bytes 580
  10.2 115.5 %copy-start.15 = (f32[48]{0:T(128)}, f32[48]{0:T(128)S(1)}, u32[]{:S(2)}) copy-start(f32[48]{0:T(128)S(1)} %get-tuple-element.87) | copy-start | bytes 580
  10.2 115.5 %copy-start.17 = (f32[48]{0:T(128)}, f32[48]{0:T(128)S(1)}, u32[]{:S(2)}) copy-start(f32[48]{0:T(128)S(1)} %get-tuple-element.88) | copy-start | bytes 580
  10.2 115.5 %copy-start.19 = (f32[48]{0:T(128)}, f32[48]{0:T(128)S(1)}, u32[]{:S(2)}) copy-start(f32[48]{0:T(128)S(1)} %get-tuple-element.89) | copy-start | bytes 580
  10.2 115.5 %copy-start.21 = (f32[48]{0:T(128)}, f32[48]{0:T(128)S(1)}, u32[]{:S(2)}) copy-start(f32[48]{0:T(128)S(1)} %get-tuple-element.90) | copy-start | bytes 580
  11.3 13.1 %copy-start.68 = (f32[48]{0:T(128)}, f32[48]{0:T(128)S(1)}, u32[]{:S(2)}) copy-start(f32[48]{0:T(128)S(1)} %get-tuple-element.106) | copy-start | bytes 580
  11.3 13.1 %copy-start.71 = (f32[48]{0:T(128)}, f32[48]{0:T(128)S(1)}, u32[]{:S(2)}) copy-start(f32[48]{0:T(128)S(1)} %get-tuple-element.107) | copy-start | bytes 580
  11.3 13.1 %copy-start.74 = (f32[48]{0:T(128)}, f32[48]{0:T(128)S(1)}, u32[]{:S(2)}) copy-start(f32[48]{0:T(128)S(1)} %get-tuple-element.108) | copy-start | bytes 580
  11.3 13.1 %copy-start.77 = (f32[48]{0:T(128)}, f32[48]{0:T(128)S(1)}, u32[]{:S(2)}) copy-start(f32[48]{0:T(128)S(1)} %get-tuple-element.109) | copy-start | bytes 580
  11.3 13.1 %copy-start.80 = (f32[48]{0:T(128)}, f32[48]{0:T(128)S(1)}, u32[]{:S(2)}) copy-start(f32[48]{0:T(128)S(1)} %get-tuple-element.110) | copy-start | bytes 580
  11.3 13.1 %copy-start.83 = (f32[48]{0:T(128)}, f32[48]{0:T(128)S(1)}, u32[]{:S(2)}) copy-start(f32[48]{0:T(128)S(1)} %get-tuple-element.111) | copy-start | bytes 580
  11.3 13.1 %copy-start.86 = (f32[48]{0:T(128)}, f32[48]{0:T(128)S(1)}, u32[]{:S(2)}) copy-start(f32[48]{0:T(128)S(1)} %get-tuple-element.112) | copy-start | bytes 580
  11.3 13.1 %copy-start.89 = (f32[48]{0:T(128)}, f32[48]{0:T(128)S(1)}, u32[]{:S(2)}) copy-start(f32[48]{0:T(128)S(1)} %get-tuple-element.113) | copy-start | bytes 580
  11.3 13.1 %copy-start.92 = (f32[48]{0:T(128)}, f32[48]{0:T(128)S(1)}, u32[]{:S(2)}) copy-start(f32[48]{0:T(128)S(1)} %get-tuple-element.114) | copy-start | bytes 580
  11.4 13.1 %copy-start.95 = (f32[48]{0:T(128)}, f32[48]{0:T(128)S(1)}, u32[]{:S(2)}) copy-start(f32[48]{0:T(128)S(1)} %get-tuple-element.115) | copy-start | bytes 580
  11.4 13.1 %copy-start.98 = (f32[48]{0:T(128)}, f32[48]{0:T(128)S(1)}, u32[]{:S(2)}) copy-start(f32[48]{0:T(128)S(1)} %get-tuple-element.116) | copy-start | bytes 580
  11.4 13.1 %copy-start.101 = (f32[48]{0:T(128)}, f32[48]{0:T(128)S(1)}, u32[]{:S(2)}) copy-start(f32[48]{0:T(128)S(1)} %get-tuple-element.117) | copy-start | bytes 580
  11.4 13.1 %copy-start.104 = (f32[48]{0:T(128)}, f32[48]{0:T(128)S(1)}, u32[]{:S(2)}) copy-start(f32[48]{0:T(128)S(1)} %get-tuple-element.118) | copy-start | bytes 580
  11.4 13.1 %copy-start.107 = (f32[48]{0:T(128)}, f32[48]{0:T(128)S(1)}, u32[]{:S(2)}) copy-start(f32[48]{0:T(128)S(1)} %get-tuple-element.119) | copy-start | bytes 580
  11.4 13.1 %copy-start.110 = (f32[48]{0:T(128)}, f32[48]{0:T(128)S(1)}, u32[]{:S(2)}) copy-start(f32[48]{0:T(128)S(1)} %get-tuple-element.120) | copy-start | bytes 580
  11.4 13.1 %copy-start.113 = (f32[48]{0:T(128)}, f32[48]{0:T(128)S(1)}, u32[]{:S(2)}) copy-start(f32[48]{0:T(128)S(1)} %get-tuple-element.121) | copy-start | bytes 580
  11.4 13.1 %copy-start.116 = (f32[48]{0:T(128)}, f32[48]{0:T(128)S(1)}, u32[]{:S(2)}) copy-start(f32[48]{0:T(128)S(1)} %get-tuple-element.122) | copy-start | bytes 580
  11.4 13.1 %copy-start.119 = (f32[48]{0:T(128)}, f32[48]{0:T(128)S(1)}, u32[]{:S(2)}) copy-start(f32[48]{0:T(128)S(1)} %get-tuple-element.123) | copy-start | bytes 580
  11.4 13.1 %copy-start.122 = (f32[48]{0:T(128)}, f32[48]{0:T(128)S(1)}, u32[]{:S(2)}) copy-start(f32[48]{0:T(128)S(1)} %get-tuple-element.124) | copy-start | bytes 580
  15.4 48.1 %copy-start.4 = (bf16[192,768]{1,0:T(8,128)(2,1)S(1)}, bf16[192,768]{1,0:T(8,128)(2,1)}, u32[]{:S(2)}) copy-start(bf16[192,768]{1,0:T(8,128)(2,1)} %param.11) | copy-start | bytes 884740
  15.4 48.1 %copy-start.5 = (bf16[768,192]{0,1:T(8,128)(2,1)S(1)}, bf16[768,192]{0,1:T(8,128)(2,1)}, u32[]{:S(2)}) copy-start(bf16[768,192]{0,1:T(8,128)(2,1)} %param.10) | copy-start | bytes 884740
  64.7 3.2 %collective-permute-start.1 = (bf16[2,384,768]{2,1,0:T(8,128)(2,1)}, bf16[2,384,768]{2,1,0:T(8,128)(2,1)}, u32[]{:S(2)}, u32[]{:S(2)}) collective-permute-start(bf16[2,384,768]{2,1,0:T(8,128)(2,1)} %pad_maximum_fusion.2), channel_id=1, source_target_pairs={{0,2},{2,0},{4,6},{6,4},{8,10},{10,8},{12,14},{14,12},{16,18},{18,... | collective-permute-start | bytes 3538952 | tf_op jit(solution)/shard_map/ppermute | solution.py:181
  153.1 26.0 %collective-permute-start.7 = (bf16[2,384,768]{2,1,0:T(8,128)(2,1)}, bf16[2,384,768]{2,1,0:T(8,128)(2,1)}, u32[]{:S(2)}, u32[]{:S(2)}) collective-permute-start(bf16[2,384,768]{2,1,0:T(8,128)(2,1)} %fusion.2), channel_id=1, source_target_pairs={{0,2},{2,0},{4,6},{6,4},{8,10},{10,8},{12,14},{14,12},{16,18},{18,... | collective-permute-start | bytes 3538952 | tf_op jit(solution)/shard_map/ppermute | solution.py:181
  165.6 13.5 %copy-start.1 = (f32[1,768,768]{2,1,0:T(8,128)S(1)}, f32[1,768,768]{2,1,0:T(8,128)}, u32[]{:S(2)}) copy-start(f32[1,768,768]{2,1,0:T(8,128)} %copy-done) | copy-start | bytes 7077892
  176.4 11.4 %collective-permute-start.6 = (bf16[48,51]{0,1:T(8,128)(2,1)S(1)}, bf16[48,51]{0,1:T(8,128)(2,1)S(1)}, u32[]{:S(2)}, u32[]{:S(2)}) collective-permute-start(bf16[48,51]{0,1:T(8,128)(2,1)S(1)} %pad_maximum_fusion.4), channel_id=1, source_target_pairs={{0,1},{1,0},{2,3},{3,2},{4,5},{5,4},{6,7},{7,6},{8,9},{9,8},{10,11... | collective-permute-start | bytes 14696 | tf_op jit(solution)/shard_map/ppermute | solution.py:181
  182.1 15.7 %collective-permute-start.8 = (bf16[2,192,768]{2,1,0:T(8,128)(2,1)S(1)}, bf16[2,192,768]{2,1,0:T(8,128)(2,1)S(1)}, u32[]{:S(2)}, u32[]{:S(2)}) collective-permute-start(bf16[2,192,768]{2,1,0:T(8,128)(2,1)S(1)} %slice.1560), channel_id=1, source_target_pairs={{0,4},{2,6},{4,0},{6,2},{8,12},{10,14},{12,8},{14,10},{16,20},{18,... | collective-permute-start | bytes 1769480 | tf_op jit(solution)/shard_map/ppermute | solution.py:181
  184.6 14.9 %collective-permute-start.4 = (bf16[48,1,3,128]{3,2,1,0:T(4,128)(2,1)S(1)}, bf16[48,1,3,128]{3,2,1,0:T(4,128)(2,1)S(1)}, u32[]{:S(2)}, u32[]{:S(2)}) collective-permute-start(bf16[48,1,3,128]{3,2,1,0:T(4,128)(2,1)S(1)} %get-tuple-element.79), channel_id=1, source_target_pairs={{0,1},{2,3},{4,5},{6,7},{8,9},{10,11},{12,13},{14,15},{16,17},{18,... | collective-permute-start | bytes 110600 | tf_op jit(solution)/shard_map/ppermute | solution.py:24
  186.5 13.0 %collective-permute-start.5 = (bf16[48,1,3,128]{3,2,1,0:T(4,128)(2,1)S(1)}, bf16[48,1,3,128]{3,2,1,0:T(4,128)(2,1)S(1)}, u32[]{:S(2)}, u32[]{:S(2)}) collective-permute-start(bf16[48,1,3,128]{3,2,1,0:T(4,128)(2,1)S(1)} %get-tuple-element.80), channel_id=1, source_target_pairs={{1,0},{3,2},{5,4},{7,6},{9,8},{11,10},{13,12},{15,14},{17,16},{19,... | collective-permute-start | bytes 110600 | tf_op jit(solution)/shard_map/ppermute | solution.py:27
  189.0 10.7 %copy-start.22 = (f32[48]{0:T(128)S(1)}, f32[48]{0:T(128)}, u32[]{:S(2)}) copy-start(f32[48]{0:T(128)} %copy-done.21) | copy-start | bytes 580
  189.0 10.7 %copy-start.25 = (f32[48]{0:T(128)S(1)}, f32[48]{0:T(128)}, u32[]{:S(2)}) copy-start(f32[48]{0:T(128)} %copy-done.23) | copy-start | bytes 580
  189.0 10.7 %copy-start.28 = (f32[48]{0:T(128)S(1)}, f32[48]{0:T(128)}, u32[]{:S(2)}) copy-start(f32[48]{0:T(128)} %copy-done.26) | copy-start | bytes 580
  189.0 10.7 %copy-start.31 = (f32[48]{0:T(128)S(1)}, f32[48]{0:T(128)}, u32[]{:S(2)}) copy-start(f32[48]{0:T(128)} %copy-done.29) | copy-start | bytes 580
  189.0 10.7 %copy-start.34 = (f32[48]{0:T(128)S(1)}, f32[48]{0:T(128)}, u32[]{:S(2)}) copy-start(f32[48]{0:T(128)} %copy-done.32) | copy-start | bytes 580
  189.1 10.7 %copy-start.37 = (f32[48]{0:T(128)S(1)}, f32[48]{0:T(128)}, u32[]{:S(2)}) copy-start(f32[48]{0:T(128)} %copy-done.35) | copy-start | bytes 580
  189.1 10.7 %copy-start.40 = (f32[48]{0:T(128)S(1)}, f32[48]{0:T(128)}, u32[]{:S(2)}) copy-start(f32[48]{0:T(128)} %copy-done.38) | copy-start | bytes 580
  189.1 10.7 %copy-start.43 = (f32[48]{0:T(128)S(1)}, f32[48]{0:T(128)}, u32[]{:S(2)}) copy-start(f32[48]{0:T(128)} %copy-done.41) | copy-start | bytes 580
  189.1 10.7 %copy-start.46 = (f32[48]{0:T(128)S(1)}, f32[48]{0:T(128)}, u32[]{:S(2)}) copy-start(f32[48]{0:T(128)} %copy-done.44) | copy-start | bytes 580
  189.1 10.7 %copy-start.49 = (f32[48]{0:T(128)S(1)}, f32[48]{0:T(128)}, u32[]{:S(2)}) copy-start(f32[48]{0:T(128)} %copy-done.47) | copy-start | bytes 580
  199.1 14.4 %collective-permute-start.9 = (bf16[2,192,768]{2,1,0:T(8,128)(2,1)S(1)}, bf16[2,192,768]{2,1,0:T(8,128)(2,1)S(1)}, u32[]{:S(2)}, u32[]{:S(2)}) collective-permute-start(bf16[2,192,768]{2,1,0:T(8,128)(2,1)S(1)} %fusion.20), channel_id=1, source_target_pairs={{0,1},{1,0},{2,3},{3,2},{4,5},{5,4},{6,7},{7,6},{8,9},{9,8},{10,11... | collective-permute-start | bytes 1769480 | tf_op jit(solution)/shard_map/ppermute | solution.py:181
  (80 other events, 481.3 us)

commit v2 on v1

v2 whole, which is shorter than its diff:
```python
import functools

import jax
import jax.numpy as jnp
from jax import lax
from jax.experimental import pallas as pl
from jax.experimental.pallas import tpu as pltpu
from jax.sharding import PartitionSpec as P

D = 768
KSIZE = 7


epsilon = 1e-06
inv_root_two = 0.7071067811865476
inv_root_two_pi = 0.3989422804014327


def extended(block, axis):
    count = lax.axis_size(axis)
    forward = [(i, i + 1) for i in range(count - 1)]
    backward = [(target, source) for source, target in forward]
    low = lax.ppermute(block[-3:], axis, forward)
    high = lax.ppermute(block[:3], axis, backward)
    return jnp.concatenate([low, block, high], axis=0)


def gelu_slope(values):
    return (
        0.5 * (1.0 + lax.erf(values * inv_root_two))
        + values * jnp.exp(-0.5 * values * values) * inv_root_two_pi
    )


GROUP = 4
MESH = pl.DeviceIdType.MESH


def greet(n, me):
    barrier = pltpu.get_barrier_semaphore()
    for k in range(1, n):
        pl.semaphore_signal(
            barrier, inc=1, device_id={"chan": lax.rem(me + k, n)}, device_id_type=MESH
        )
    pl.semaphore_wait(barrier, n - 1)


def spread_kernel(n, part, *refs):
    count = (len(refs) - 3) // 2
    sources, targets = refs[:count], refs[count : 2 * count]
    local_sem, send_sem, recv_sem = refs[2 * count :]
    me = lax.axis_index("chan")
    greet(n, me)

    def piece(ref, peer):
        if ref.shape[0] == part * GROUP:
            return ref.at[pl.ds(lax.rem(peer, GROUP) * part, part)]
        return ref

    copies = []
    for k in range(1, n):
        peer = lax.rem(me + k, n)
        for a in range(count):
            copy = pltpu.make_async_remote_copy(
                src_ref=piece(sources[a], peer),
                dst_ref=targets[a].at[:, me],
                send_sem=send_sem.at[a, k],
                recv_sem=recv_sem.at[a, k],
                device_id={"chan": peer},
                device_id_type=MESH,
            )
            copy.start()
            copies.append(copy)
    own = []
    for a in range(count):
        copy = pltpu.make_async_copy(piece(sources[a], me), targets[a].at[:, me], local_sem.at[a])
        copy.start()
        own.append(copy)
    for copy in own + copies:
        copy.wait()


def collect_kernel(n, part, *refs):
    count = (len(refs) - 3) // 2
    sources, targets = refs[:count], refs[count : 2 * count]
    local_sem, send_sem, recv_sem = refs[2 * count :]
    me = lax.axis_index("chan")
    plane = lax.div(me, GROUP)
    greet(n, me)
    lines = pl.ds(lax.rem(me, GROUP) * part, part)

    def piece(ref, peer):
        return ref.at[:, peer] if len(ref.shape) == 4 else ref

    copies = []
    for k in range(1, n):
        peer = lax.rem(me + k, n)
        for a in range(count):
            copy = pltpu.make_async_remote_copy(
                src_ref=piece(sources[a], peer),
                dst_ref=targets[a].at[plane, lines],
                send_sem=send_sem.at[a, k],
                recv_sem=recv_sem.at[a, k],
                device_id={"chan": peer},
                device_id_type=MESH,
            )
            copy.start()
            copies.append(copy)
    own = []
    for a in range(count):
        copy = pltpu.make_async_copy(
            piece(sources[a], me), targets[a].at[plane, lines], local_sem.at[a]
        )
        copy.start()
        own.append(copy)
    for copy in own + copies:
        copy.wait()


def exchange(kernel, identity, arrays, shapes, n, part):
    count = len(arrays)
    size = sum(a.size * a.dtype.itemsize for a in arrays)
    return pl.pallas_call(
        functools.partial(kernel, n, part),
        out_shape=tuple(
            jax.ShapeDtypeStruct(shape, a.dtype) for shape, a in zip(shapes, arrays)
        ),
        in_specs=[pl.BlockSpec(memory_space=pl.ANY)] * count,
        out_specs=tuple([pl.BlockSpec(memory_space=pl.ANY)] * count),
        scratch_shapes=[
            pltpu.SemaphoreType.DMA((count,)),
            pltpu.SemaphoreType.DMA((count, n)),
            pltpu.SemaphoreType.DMA((count, n)),
        ],
        compiler_params=pltpu.CompilerParams(collective_id=identity, has_side_effects=True),
        cost_estimate=pl.CostEstimate(flops=0, bytes_accessed=100 * size, transcendentals=0),
    )(*arrays)


def swap(value, axis, bit):
    n = lax.axis_size(axis)
    return lax.ppermute(value, axis, [(i, i ^ bit) for i in range(n)])


def total_over(value, axis):
    bit = 1
    while bit < lax.axis_size(axis):
        near = value.astype(jnp.bfloat16)
        value = near.astype(jnp.float32) + swap(near, axis, bit).astype(jnp.float32)
        bit *= 2
    return value


def shifted(value, shift):
    if shift == 0:
        return value
    breadth = value.shape[1]
    lane = lax.broadcasted_iota(jnp.int32, value.shape, 1)
    rolled = pltpu.roll(value, shift % breadth, 1)
    keep = lane >= shift if shift > 0 else lane < breadth + shift
    return jnp.where(keep, rolled, 0.0)


def forward_kernel(padded_ref, taps_ref, mixed_ref):
    height = mixed_ref.shape[0]
    taps = taps_ref[...]
    sums = [None] * height
    for v in range(KSIZE):
        lines = [shifted(padded_ref[r], 3 - v) for r in range(height + 6)]
        for u in range(KSIZE):
            t = u * KSIZE + v
            tap = jnp.broadcast_to(taps[:, t : t + 1], lines[0].shape)
            for r in range(height):
                term = tap * lines[r + u]
                sums[r] = term if sums[r] is None else sums[r] + term
    for r in range(height):
        mixed_ref[r] = sums[r].astype(mixed_ref.dtype)


def backward_kernel(grad_ref, padded_ref, taps_ref, cotan_ref, image_grad_ref, taps_grad_ref):
    height = cotan_ref.shape[0]
    taps = taps_ref[...]
    lane = lax.broadcasted_iota(jnp.int32, taps.shape, 1)
    taps_grad = jnp.zeros_like(taps)
    sums = [None] * height
    for v in range(KSIZE):
        lines = [shifted(grad_ref[r], v - 3) for r in range(height + 6)]
        for u in range(KSIZE):
            t = u * KSIZE + v
            tap = jnp.broadcast_to(taps[:, t : t + 1], lines[0].shape)
            for r in range(height):
                term = tap * lines[r + 6 - u]
                sums[r] = term if sums[r] is None else sums[r] + term
            both = [lines[r + 3] * padded_ref[r + u] for r in range(height)]
            while len(both) > 1:
                both = [p + q for p, q in zip(both[::2], both[1::2])] + both[len(both) // 2 * 2 :]
            taps_grad = jnp.where(lane == t, jnp.sum(both[0], axis=1, keepdims=True), taps_grad)
    for r in range(height):
        image_grad_ref[r] = (sums[r] + cotan_ref[r].astype(jnp.float32)).astype(
            image_grad_ref.dtype
        )
    taps_grad_ref[...] = taps_grad


def stencil(kernel, arrays, outs):
    channels = arrays[0].shape[1]

    def spec(value):
        if len(value.shape) == 2:
            return pl.BlockSpec((8, value.shape[1]), lambda i: (i, 0))
        return pl.BlockSpec((value.shape[0], 8, value.shape[2]), lambda i: (0, i, 0))

    return pl.pallas_call(
        kernel,
        grid=(channels // 8,),
        out_shape=tuple(outs),
        in_specs=[spec(a) for a in arrays],
        out_specs=tuple(spec(o) for o in outs),
        cost_estimate=pl.CostEstimate(
            flops=10000000, bytes_accessed=6000000, transcendentals=0
        ),
    )(*arrays)


def body(image, dw_kernel, ln_gain, w_in, w_out, layer_scale, cotangent):
    channels, images, height, breadth = image.shape
    part = height // GROUP
    n = lax.axis_size("chan")
    every = n * channels
    planes = n // GROUP
    contract_lead = (((0,), (0,)), ((), ()))
    contract_tail = (((1,), (1,)), ((), ()))
    bf16, f32 = jnp.bfloat16, jnp.float32
    image_rows = jnp.transpose(image[:, 0], (1, 0, 2))
    cotan_rows = jnp.transpose(cotangent[:, 0], (1, 0, 2))
    taps = jnp.pad(dw_kernel.reshape(channels, KSIZE * KSIZE), ((0, 0), (0, 128 - KSIZE * KSIZE)))
    padded = extended(image_rows, "rows").astype(f32)
    weights = jnp.stack([w_in.T, w_out])
    weights = jnp.concatenate([weights, swap(weights, "chan", 2)], axis=1)
    weights = jnp.concatenate([weights, swap(weights, "chan", 1)], axis=1)
    (mixed_in,) = stencil(
        forward_kernel, (padded, taps), (jax.ShapeDtypeStruct(image_rows.shape, bf16),)
    )
    scaled = (layer_scale[:, None] * cotan_rows.astype(f32)).astype(bf16)
    gain_row = jnp.pad(ln_gain[None, None, :], ((0, 0), (0, 0), (0, 128 - channels)))
    mixed_all, scaled_all, gain_all = exchange(
        spread_kernel,
        0,
        (mixed_in, scaled, gain_row),
        ((part, n, channels, breadth), (part, n, channels, breadth), (1, n, 1, 128)),
        n,
        part,
    )

    def flat(value):
        value = value.reshape(part, every, breadth)
        return jnp.concatenate([value[i] for i in range(part)], axis=1)

    def split(value):
        value = jnp.stack([value[:, i * breadth : (i + 1) * breadth] for i in range(part)])
        return value.reshape(part, n, channels, breadth)

    mixed_all = flat(mixed_all).astype(f32)
    scaled_all = flat(scaled_all)
    gain_all = gain_all[0, :, 0, :channels].reshape(every, 1)
    centre = jnp.mean(mixed_all, axis=0)
    spread = jnp.mean(jnp.square(mixed_all - centre), axis=0)
    inv_scale = lax.rsqrt(spread + epsilon)
    unit_all = (mixed_all - centre) * inv_scale
    normed = (unit_all * gain_all).astype(bf16)
    pre_act = jnp.dot(weights[0], normed, preferred_element_type=f32)
    grad_act = jnp.dot(weights[1], scaled_all, preferred_element_type=f32)
    activated = jax.nn.gelu(pre_act, approximate=False).astype(bf16)
    grad_pre = (grad_act * gelu_slope(pre_act)).astype(bf16)
    branch_part = lax.dot_general(
        weights[1], activated, contract_lead, preferred_element_type=f32
    ).astype(bf16)
    normed_part = lax.dot_general(weights[0], grad_pre, contract_lead, preferred_element_type=f32)
    gained_part = normed_part * gain_all
    stats = jnp.stack(
        [jnp.sum(gained_part, axis=0), jnp.sum(gained_part * unit_all, axis=0), centre, inv_scale]
    )
    stats = jnp.transpose(stats.reshape(4, part, breadth), (1, 0, 2))
    grad_w_in = lax.dot_general(grad_pre, normed, contract_tail, preferred_element_type=f32)
    grad_w_out = lax.dot_general(activated, scaled_all, contract_tail, preferred_element_type=f32)
    branch_all, normed_all, stats_all = exchange(
        collect_kernel,
        1,
        (split(branch_part), split(normed_part.astype(bf16)), stats),
        (
            (planes, height, channels, breadth),
            (planes, height, channels, breadth),
            (planes, height, 4, breadth),
        ),
        n,
        part,
    )
    grads = jnp.stack([grad_w_in, grad_w_out])
    for bit in (1, 2):
        half = grads.shape[1] // 2
        grads = grads[:, :half] + swap(grads[:, half:].astype(bf16), "chan", bit).astype(f32)
    grads = total_over(grads, "rows")
    branch = jnp.sum(branch_all.astype(f32), axis=0)
    grad_normed = jnp.sum(normed_all.astype(f32), axis=0)
    total_one = jnp.sum(stats_all[:, :, 0:1], axis=0)
    total_two = jnp.sum(stats_all[:, :, 1:2], axis=0)
    centre, inv_scale = stats_all[0, :, 2:3], stats_all[0, :, 3:4]
    unit_norm = (mixed_in.astype(f32) - centre) * inv_scale
    scaled_grad = grad_normed * ln_gain[:, None]
    grad_mixed = (inv_scale * (scaled_grad - total_one / D - unit_norm * (total_two / D))).astype(
        bf16
    )
    rimmed_grad = extended(grad_mixed, "rows").astype(f32)
    image_grad, grad_kernel = stencil(
        backward_kernel,
        (rimmed_grad, padded, taps, cotan_rows),
        (
            jax.ShapeDtypeStruct(image_rows.shape, bf16),
            jax.ShapeDtypeStruct((channels, 128), f32),
        ),
    )
    block_out = (image_rows.astype(f32) + layer_scale[:, None] * branch).astype(bf16)
    grad_scale = jnp.sum(cotan_rows.astype(f32) * branch, axis=(0, 2))
    grad_gain = jnp.sum(grad_normed * unit_norm, axis=(0, 2))
    small = jnp.concatenate(
        [grad_kernel[:, : KSIZE * KSIZE], grad_gain[:, None], grad_scale[:, None]], axis=1
    )
    small = total_over(small, "rows")
    grad_kernel = small[:, : KSIZE * KSIZE].reshape(channels, KSIZE, KSIZE)
    return (
        jnp.transpose(block_out, (1, 0, 2))[:, None],
        jnp.transpose(image_grad, (1, 0, 2))[:, None],
        grad_kernel,
        small[:, KSIZE * KSIZE],
        small[:, KSIZE * KSIZE + 1],
        grads[0].T,
        grads[1],
    )


def solution(mesh):
    return jax.shard_map(
        body,
        mesh=mesh,
        in_specs=(
            P("chan", None, "rows", None),
            P("chan", None, None),
            P("chan"),
            P(None, "chan"),
            P("chan", None),
            P("chan"),
            P("chan", None, "rows", None),
        ),
        out_specs=(
            P("chan", None, "rows", None),
            P("chan", None, "rows", None),
            P("chan", None, None),
            P("chan"),
            P("chan"),
            P(None, "chan"),
            P("chan", None),
        ),
        check_vma=False,
    )
```

time: 216 us -> 170 us (0.79)
  the two profiles are of different devices: /device:TPU:8 before, /device:TPU:12 now
where the time goes in v2:
time: 170 us
  Pallas kernels  95.2 us (56%)
  waiting for transfers between devices  22 us (13%)
  other arithmetic  15.7 us (9%)
  local copies, waits for them, and re-layouts  15.4 us (9%)
  starting transfers between devices  11.8 us (7%)
  matrix products  8.61 us (5%)
    pallas_call x2, Pallas kernels, exchange(): pl.pallas_call(functools.partial(kernel, n, part), out_shape=tuple((jax.S...  81.6 us
    ppermute x6, waiting for transfers between devices, swap(): return lax.ppermute(value, axis, [(i, i ^ bit) for i in range(n)])  18.4 us
    pallas_call x2, Pallas kernels, stencil(): pl.pallas_call(kernel, grid=(channels // 8,), out_shape=tuple(outs), in_s...  13.6 us
    unnamed x32, local copies, waits for them, and re-layouts  5.73 us
    ppermute x2, starting transfers between devices, extended(): high = lax.ppermute(block[:3], axis, backward)  4.82 us
    ppermute x6, starting transfers between devices, swap(): return lax.ppermute(value, axis, [(i, i ^ bit) for i in range(n)])  4.35 us
    dot_general x1, matrix products, body(): pre_act = jnp.dot(weights[0], normed, preferred_element_type=f32)  3.99 us
    ppermute x2, waiting for transfers between devices, extended(): low = lax.ppermute(block[-3:], axis, forward)  3.6 us
  transfers between devices with their start and end apart: 10, of which 3 were waited for; matrix products, arithmetic and copies ran while one was open for 11% of the time, Pallas kernels for 56%

profile of v2, /device:TPU:12, one launch (start us, length us, event | category | flops | bytes accessed | tf_op | source)
XLA Modules:
  0.0 169.7 jit_solution(11268946889677834554)
XLA Ops:
  0.7 1.2 pad_maximum_fusion.7
  1.9 1.6 collective-permute-start
  3.4 1.0 copy.38
  4.4 2.4 %collective-permute-start.3 = (bf16[3,48,128]{2,1,0:T(8,128)(2,1)S(1)}, bf16[3,48,128]{2,1,0:T(8,128)(2,1)S(1)}, u32[]{:S(2)}, u32[]{:S(2)}) collective-permute-start(bf16[3,48,128]{2,1,0:T(8,128)(2,1)S(1)} %get-tuple-element.67), channel_id=1, source_target_pairs={{1,0},{3,2},{5,4},{7,6},{9,8},{11,10},{13,12},{15,14},{17,16},{19,... | collective-permute-start | bytes 110600 | tf_op jit(solution)/shard_map/ppermute | solution.py:24
  6.8 1.3 collective-permute-start.2
  8.2 0.1 copy.23
  8.2 0.6 pad.8.taps_ref
  8.9 0.5 pad.9.refs_2_
  9.4 0.7 copy.37
  10.1 0.8 fusion.29.refs_1_
  10.9 6.1 %collective-permute-done = bf16[2,192,768]{2,1,0:T(8,128)(2,1)S(1)} collective-permute-done((bf16[2,192,768]{2,1,0:T(8,128)(2,1)S(1)}, bf16[2,192,768]{2,1,0:T(8,128)(2,1)S(1)}, u32[]{:S(2)}, u32[]{:S(2)}) %collective-permute-start) | collective-permute-done | bytes 589856 | tf_op jit(solution)/shard_map/ppermute | solution.py:142
  17.2 0.8 maximum_convert_fusion.padded_ref
  18.0 5.0 %shard_map.126.refs_0_ = bf16[16,48,128]{2,1,0:T(8,128)(2,1)} custom-call(f32[22,48,128]{2,1,0:T(8,128)} %maximum_convert_fusion.padded_ref, f32[48,128]{1,0:T(8,128)} %pad.8.taps_ref), custom_call_target="tpu_custom_call" | custom-call | flops 10000000 | bytes 6000000 | tf_op jit(solution)/shard_map/pallas_call | solution.py:213
  23.0 39.3 %shard_map.127 = (bf16[4,16,48,128]{3,2,1,0:T(8,128)(2,1)}, bf16[4,16,48,128]{3,2,1,0:T(8,128)(2,1)}, f32[1,16,1,128]{3,2,1,0:T(1,128)}) custom-call(bf16[16,48,128]{2,1,0:T(8,128)(2,1)} %shard_map.126.refs_0_, bf16[16,48,128]{2,1,0:T(8,128)(2,1)} %fusion.29.refs_1_, f32[1,1,128]{2,1,0:T(1,128)} %pad.9.refs_2_), custom_call_target="tpu_custom_call" | custom-call | bytes 39372800 | tf_op jit(solution)/shard_map/pallas_call | solution.py:123
  62.3 0.7 slice_reduce_fusion.4
  63.1 1.6 fusion.38
  64.7 0.2 convert_reduce_fusion
  64.9 0.3 fusion.9
  65.1 1.4 pad_maximum_fusion.1
  66.6 4.0 %fusion.12 = (bf16[768,512]{1,0:T(8,128)(2,1)S(1)}, f32[768,512]{1,0:T(8,128)S(1)}) fusion(f32[768]{0:T(1024)S(1)} %mul.123, f32[512]{0:T(512)S(1)} %add_rsqrt_fusion, f32[512]{0:T(512)S(1)} %broadcast_multiply_fusion.2, bf16[768,128]{1,0:T(8,128)(2,1)S(1)} %bitcast.110, bf16[768,128]{1,0:T(8,128)(2,1)S(1)} %bitcast.105, ...), kind=kOutput, calls=%fused_computation.22 | convolution fusion | flops 634257408 | bytes 4333568 | tf_op jit(solution)/shard_map/dot_general | solution.py:271
  70.6 1.1 fusion.18
  71.7 1.0 multiply_reduce_fusion
  72.7 0.9 convolution_bitcast_fusion.1
  73.6 0.8 convolution_convert_fusion
  74.4 0.8 convolution_bitcast_fusion
  75.2 0.1 fusion.39
  75.4 0.1 fusion.37
  75.5 1.1 copy-done
  76.6 1.2 fusion.2
  77.8 1.0 pad_maximum_fusion.4.refs_0_
  78.9 1.0 pad_maximum_fusion.6.refs_1_
  79.8 0.6 maximum_bitcast_fusion.refs_2_
  80.5 42.4 %shard_map.128 = (bf16[4,16,48,128]{3,2,1,0:T(8,128)(2,1)}, bf16[4,16,48,128]{3,2,1,0:T(8,128)(2,1)}, f32[4,16,4,128]{3,2,1,0:T(4,128)}) custom-call(bf16[4,16,48,128]{3,2,1,0:T(8,128)(2,1)} %pad_maximum_fusion.4.refs_0_, bf16[4,16,48,128]{3,2,1,0:T(8,128)(2,1)} %pad_maximum_fusion.6.refs_1_, f32[4,4,128]{2,1,0:T(4,128)} %maximum_bitcast_fusion.refs_2_), custom_call_target="tpu_custom_call" | custom-call | bytes 158105600 | tf_op jit(solution)/shard_map/pallas_call | solution.py:123
  122.8 1.1 slice_reduce_fusion.1
  123.9 1.3 convert_reduce_fusion.1
  125.2 0.9 fusion.43
  126.1 0.2 multiply_reduce_fusion.1
  126.3 1.9 %fusion.1 = f32[2,384,768]{2,1,0:T(8,128)S(1)} fusion(f32[1,768,768]{2,1,0:T(8,128)S(1)} %convolution_bitcast_fusion.1, f32[1,768,768]{2,1,0:T(8,128)} %copy-done, bf16[2,384,768]{2,1,0:T(8,128)(2,1)} %collective-permute-done.7), kind=kLoop, calls=%fused_computation.5 | loop fusion | flops 1769472 | bytes 8257536 | tf_op jit(solution)/shard_map/add | solution.py:301
  128.2 1.4 copy-done.1
  129.6 0.9 slice.211
  130.4 0.6 collective-permute-start.8
  131.1 2.4 %collective-permute-start.5 = (bf16[3,48,128]{2,1,0:T(8,128)(2,1)S(1)}, bf16[3,48,128]{2,1,0:T(8,128)(2,1)S(1)}, u32[]{:S(2)}, u32[]{:S(2)}) collective-permute-start(bf16[3,48,128]{2,1,0:T(8,128)(2,1)S(1)} %get-tuple-element.65), channel_id=1, source_target_pairs={{1,0},{3,2},{5,4},{7,6},{9,8},{11,10},{13,12},{15,14},{17,16},{19,... | collective-permute-start | bytes 110600 | tf_op jit(solution)/shard_map/ppermute | solution.py:24
  133.5 1.3 collective-permute-start.4
  134.8 0.1 convert_reduce_fusion.2
  134.9 0.2 fusion.30
  135.1 0.1 copy.26
  135.2 0.7 copy.25
  135.9 3.6 %collective-permute-done.4 = bf16[3,48,128]{2,1,0:T(8,128)(2,1)S(1)} collective-permute-done((bf16[3,48,128]{2,1,0:T(8,128)(2,1)S(1)}, bf16[3,48,128]{2,1,0:T(8,128)(2,1)S(1)}, u32[]{:S(2)}, u32[]{:S(2)}) %collective-permute-start.4) | collective-permute-done | bytes 36896 | tf_op jit(solution)/shard_map/ppermute | solution.py:23
  139.5 0.8 maximum_convert_fusion.1.grad_ref
  140.3 8.6 %shard_map.129 = (bf16[16,48,128]{2,1,0:T(8,128)(2,1)}, f32[48,128]{1,0:T(8,128)}) custom-call(f32[22,48,128]{2,1,0:T(8,128)} %maximum_convert_fusion.1.grad_ref, f32[22,48,128]{2,1,0:T(8,128)} %maximum_convert_fusion.padded_ref, f32[48,128]{1,0:T(8,128)} %pad.8.taps_ref, bf16[16,48,128]{2,1,0:T(8,128)(2,1)} %bitcast.128), custom_call_target="tpu_custom_call" | custom-call | flops 10000000 | bytes 6000000 | tf_op jit(solution)/shard_map/pallas_call | solution.py:213
  148.9 0.8 slice.212
  149.7 1.2 fusion.26
  151.0 0.1 pad_maximum_fusion.10
  151.1 2.0 %collective-permute-start.6 = (bf16[48,51]{1,0:T(8,128)(2,1)S(1)}, bf16[48,51]{1,0:T(8,128)(2,1)S(1)}, u32[]{:S(2)}, u32[]{:S(2)}) collective-permute-start(bf16[48,51]{1,0:T(8,128)(2,1)S(1)} %pad_maximum_fusion.10), channel_id=1, source_target_pairs={{0,1},{1,0},{2,3},{3,2},{4,5},{5,4},{6,7},{7,6},{8,9},{9,8},{10,11... | collective-permute-start | bytes 14696 | tf_op jit(solution)/shard_map/ppermute | solution.py:142
  153.1 0.1 fusion.32
  153.2 0.7 copy.28
  154.0 0.7 copy.29
  154.7 12.2 %collective-permute-done.6 = bf16[48,51]{1,0:T(8,128)(2,1)S(1)} collective-permute-done((bf16[48,51]{1,0:T(8,128)(2,1)S(1)}, bf16[48,51]{1,0:T(8,128)(2,1)S(1)}, u32[]{:S(2)}, u32[]{:S(2)}) %collective-permute-start.6) | collective-permute-done | bytes 4928 | tf_op jit(solution)/shard_map/ppermute | solution.py:142
  166.9 0.1 convert_add_fusion.1
  167.0 0.1 copy.27
  167.1 0.6 reshape.120
  167.7 0.7 slice_reduce_fusion.2
  168.4 0.1 convert_add_fusion
  168.6 1.1 slice_bitcast_fusion.6
  (45 shorter events, 0.4 us)
Async XLA Ops:
  0.6 16.4 %copy-start.3 = (bf16[192,768]{1,0:T(8,128)(2,1)S(1)}, bf16[192,768]{1,0:T(8,128)(2,1)}, u32[]{:S(2)}) copy-start(bf16[192,768]{1,0:T(8,128)(2,1)} %param.11) | copy-start | bytes 884740
  0.6 16.4 %copy-start.4 = (bf16[768,192]{0,1:T(8,128)(2,1)S(1)}, bf16[768,192]{0,1:T(8,128)(2,1)}, u32[]{:S(2)}) copy-start(bf16[768,192]{0,1:T(8,128)(2,1)} %param.10) | copy-start | bytes 884740
  0.7 7.5 %copy-start.11 = (f32[48,7,7]{0,2,1:T(8,128)S(1)}, f32[48,7,7]{0,2,1:T(8,128)}, u32[]{:S(2)}) copy-start(f32[48,7,7]{0,2,1:T(8,128)} %param.8) | copy-start | bytes 28228
  0.7 8.2 %copy-start.13 = (f32[48]{0:T(128)S(1)}, f32[48]{0:T(128)}, u32[]{:S(2)}) copy-start(f32[48]{0:T(128)} %param.9) | copy-start | bytes 580
  0.7 8.7 %copy-start.5 = (bf16[48,1,16,128]{3,2,1,0:T(8,128)(2,1)S(1)}, bf16[48,1,16,128]{3,2,1,0:T(8,128)(2,1)}, u32[]{:S(2)}) copy-start(bf16[48,1,16,128]{3,2,1,0:T(8,128)(2,1)} %param.13) | copy-start | bytes 589828
  0.7 9.4 %copy-start.12 = (f32[48]{0:T(128)S(1)}, f32[48]{0:T(128)}, u32[]{:S(2)}) copy-start(f32[48]{0:T(128)} %param.12) | copy-start | bytes 580
  1.9 15.1 %collective-permute-start = (bf16[2,192,768]{2,1,0:T(8,128)(2,1)S(1)}, bf16[2,192,768]{2,1,0:T(8,128)(2,1)S(1)}, u32[]{:S(2)}, u32[]{:S(2)}) collective-permute-start(bf16[2,192,768]{2,1,0:T(8,128)(2,1)S(1)} %pad_maximum_fusion.7), channel_id=1, source_target_pairs={{0,4},{2,6},{4,0},{6,2},{8,12},{10,14},{12,8},{14,10},{16,20},{18,... | collective-permute-start | bytes 1769480 | tf_op jit(solution)/shard_map/ppermute | solution.py:142
  4.4 12.8 %collective-permute-start.3 = (bf16[3,48,128]{2,1,0:T(8,128)(2,1)S(1)}, bf16[3,48,128]{2,1,0:T(8,128)(2,1)S(1)}, u32[]{:S(2)}, u32[]{:S(2)}) collective-permute-start(bf16[3,48,128]{2,1,0:T(8,128)(2,1)S(1)} %get-tuple-element.67), channel_id=1, source_target_pairs={{1,0},{3,2},{5,4},{7,6},{9,8},{11,10},{13,12},{15,14},{17,16},{19,... | collective-permute-start | bytes 110600 | tf_op jit(solution)/shard_map/ppermute | solution.py:24
  6.8 10.3 %collective-permute-start.2 = (bf16[3,48,128]{2,1,0:T(8,128)(2,1)S(1)}, bf16[3,48,128]{2,1,0:T(8,128)(2,1)S(1)}, u32[]{:S(2)}, u32[]{:S(2)}) collective-permute-start(bf16[3,48,128]{2,1,0:T(8,128)(2,1)S(1)} %get-tuple-element.66), channel_id=1, source_target_pairs={{0,1},{2,3},{4,5},{6,7},{8,9},{10,11},{12,13},{14,15},{16,17},{18,... | collective-permute-start | bytes 110600 | tf_op jit(solution)/shard_map/ppermute | solution.py:23
  17.1 48.1 %collective-permute-start.1 = (bf16[2,384,768]{2,1,0:T(8,128)(2,1)S(1)}, bf16[2,384,768]{2,1,0:T(8,128)(2,1)}, u32[]{:S(2)}, u32[]{:S(2)}) collective-permute-start(bf16[2,384,768]{2,1,0:T(8,128)(2,1)S(1)} %pad_maximum_fusion.2), channel_id=1, source_target_pairs={{0,2},{2,0},{4,6},{6,4},{8,10},{10,8},{12,14},{14,12},{16,18},{18,... | collective-permute-start | bytes 3538952 | tf_op jit(solution)/shard_map/ppermute | solution.py:142
  75.2 1.4 copy-start
  77.8 48.5 %collective-permute-start.7 = (bf16[2,384,768]{2,1,0:T(8,128)(2,1)}, bf16[2,384,768]{2,1,0:T(8,128)(2,1)}, u32[]{:S(2)}, u32[]{:S(2)}) collective-permute-start(bf16[2,384,768]{2,1,0:T(8,128)(2,1)} %fusion.2), channel_id=1, source_target_pairs={{0,2},{2,0},{4,6},{6,4},{8,10},{10,8},{12,14},{14,12},{16,18},{18,... | collective-permute-start | bytes 3538952 | tf_op jit(solution)/shard_map/ppermute | solution.py:142
  79.8 46.2 %copy-start.6 = (bf16[16,48,128]{2,1,0:T(8,128)(2,1)S(1)}, bf16[16,48,128]{2,1,0:T(8,128)(2,1)}, u32[]{:S(2)}) copy-start(bf16[16,48,128]{2,1,0:T(8,128)(2,1)} %shard_map.126.refs_0_) | copy-start | bytes 589828
  128.2 1.4 copy-start.1
  129.6 5.2 %copy-start.7 = (bf16[4,16,48,128]{3,2,1,0:T(8,128)(2,1)S(1)}, bf16[4,16,48,128]{3,2,1,0:T(8,128)(2,1)}, u32[]{:S(2)}) copy-start(bf16[4,16,48,128]{3,2,1,0:T(8,128)(2,1)} %get-tuple-element.18) | copy-start | bytes 2359300
  130.4 19.3 %collective-permute-start.8 = (bf16[2,192,768]{2,1,0:T(8,128)(2,1)}, bf16[2,192,768]{2,1,0:T(8,128)(2,1)}, u32[]{:S(2)}, u32[]{:S(2)}) collective-permute-start(bf16[2,192,768]{2,1,0:T(8,128)(2,1)} %slice.211), channel_id=1, source_target_pairs={{0,4},{2,6},{4,0},{6,2},{8,12},{10,14},{12,8},{14,10},{16,20},{18,... | collective-permute-start | bytes 1769480 | tf_op jit(solution)/shard_map/ppermute | solution.py:142
  131.1 4.8 %collective-permute-start.5 = (bf16[3,48,128]{2,1,0:T(8,128)(2,1)S(1)}, bf16[3,48,128]{2,1,0:T(8,128)(2,1)S(1)}, u32[]{:S(2)}, u32[]{:S(2)}) collective-permute-start(bf16[3,48,128]{2,1,0:T(8,128)(2,1)S(1)} %get-tuple-element.65), channel_id=1, source_target_pairs={{1,0},{3,2},{5,4},{7,6},{9,8},{11,10},{13,12},{15,14},{17,16},{19,... | collective-permute-start | bytes 110600 | tf_op jit(solution)/shard_map/ppermute | solution.py:24
  133.5 6.0 %collective-permute-start.4 = (bf16[3,48,128]{2,1,0:T(8,128)(2,1)S(1)}, bf16[3,48,128]{2,1,0:T(8,128)(2,1)S(1)}, u32[]{:S(2)}, u32[]{:S(2)}) collective-permute-start(bf16[3,48,128]{2,1,0:T(8,128)(2,1)S(1)} %get-tuple-element.64), channel_id=1, source_target_pairs={{0,1},{2,3},{4,5},{6,7},{8,9},{10,11},{12,13},{14,15},{16,17},{18,... | collective-permute-start | bytes 110600 | tf_op jit(solution)/shard_map/ppermute | solution.py:23
  134.9 14.8 %copy-start.2 = (f32[2,384,768]{2,1,0:T(8,128)S(1)}, f32[2,384,768]{2,1,0:T(8,128)}, u32[]{:S(2)}) copy-start(f32[2,384,768]{2,1,0:T(8,128)} %copy-done.1) | copy-start | bytes 7077892
  140.3 12.8 %copy-start.8 = (bf16[48,1,16,128]{3,2,1,0:T(8,128)(2,1)S(1)}, bf16[48,1,16,128]{3,2,1,0:T(8,128)(2,1)}, u32[]{:S(2)}) copy-start(bf16[48,1,16,128]{3,2,1,0:T(8,128)(2,1)} %param.7) | copy-start | bytes 589828
  148.9 2.1 %copy-start.10 = (bf16[48,1]{1,0:T(8,128)(2,1)S(1)}, bf16[48,1]{1,0:T(8,128)(2,1)}, u32[]{:S(2)}) copy-start(bf16[48,1]{1,0:T(8,128)(2,1)} %copy.25) | copy-start | bytes 292
  149.7 4.3 %copy-start.9 = (bf16[16,48,128]{2,1,0:T(8,128)(2,1)S(1)}, bf16[16,48,128]{2,1,0:T(8,128)(2,1)}, u32[]{:S(2)}) copy-start(bf16[16,48,128]{2,1,0:T(8,128)(2,1)} %get-tuple-element.21) | copy-start | bytes 589828
  150.9 17.5 %collective-permute-start.9 = (bf16[2,192,768]{2,1,0:T(8,128)(2,1)S(1)}, bf16[2,192,768]{2,1,0:T(8,128)(2,1)S(1)}, u32[]{:S(2)}, u32[]{:S(2)}) collective-permute-start(bf16[2,192,768]{2,1,0:T(8,128)(2,1)S(1)} %fusion.26), channel_id=1, source_target_pairs={{0,1},{1,0},{2,3},{3,2},{4,5},{5,4},{6,7},{7,6},{8,9},{9,8},{10,11... | collective-permute-start | bytes 1769480 | tf_op jit(solution)/shard_map/ppermute | solution.py:142
  151.1 15.8 %collective-permute-start.6 = (bf16[48,51]{1,0:T(8,128)(2,1)S(1)}, bf16[48,51]{1,0:T(8,128)(2,1)S(1)}, u32[]{:S(2)}, u32[]{:S(2)}) collective-permute-start(bf16[48,51]{1,0:T(8,128)(2,1)S(1)} %pad_maximum_fusion.10), channel_id=1, source_target_pairs={{0,1},{1,0},{2,3},{3,2},{4,5},{5,4},{6,7},{7,6},{8,9},{9,8},{10,11... | collective-permute-start | bytes 14696 | tf_op jit(solution)/shard_map/ppermute | solution.py:142

commit v3 on v2

--- a/solution.py
+++ b/solution.py
@@ -80,43 +80,6 @@
         copy.wait()
 
 
-def collect_kernel(n, part, *refs):
-    count = (len(refs) - 3) // 2
-    sources, targets = refs[:count], refs[count : 2 * count]
-    local_sem, send_sem, recv_sem = refs[2 * count :]
-    me = lax.axis_index("chan")
-    plane = lax.div(me, GROUP)
-    greet(n, me)
-    lines = pl.ds(lax.rem(me, GROUP) * part, part)
-
-    def piece(ref, peer):
-        return ref.at[:, peer] if len(ref.shape) == 4 else ref
-
-    copies = []
-    for k in range(1, n):
-        peer = lax.rem(me + k, n)
-        for a in range(count):
-            copy = pltpu.make_async_remote_copy(
-                src_ref=piece(sources[a], peer),
-                dst_ref=targets[a].at[plane, lines],
-                send_sem=send_sem.at[a, k],
-                recv_sem=recv_sem.at[a, k],
-                device_id={"chan": peer},
-                device_id_type=MESH,
-            )
-            copy.start()
-            copies.append(copy)
-    own = []
-    for a in range(count):
-        copy = pltpu.make_async_copy(
-            piece(sources[a], me), targets[a].at[plane, lines], local_sem.at[a]
-        )
-        copy.start()
-        own.append(copy)
-    for copy in own + copies:
-        copy.wait()
-
-
 def exchange(kernel, identity, arrays, shapes, n, part):
     count = len(arrays)
     size = sum(a.size * a.dtype.itemsize for a in arrays)
@@ -140,15 +103,6 @@
 def swap(value, axis, bit):
     n = lax.axis_size(axis)
     return lax.ppermute(value, axis, [(i, i ^ bit) for i in range(n)])
-
-
-def total_over(value, axis):
-    bit = 1
-    while bit < lax.axis_size(axis):
-        near = value.astype(jnp.bfloat16)
-        value = near.astype(jnp.float32) + swap(near, axis, bit).astype(jnp.float32)
-        bit *= 2
-    return value
 
 
 def shifted(value, shift):
@@ -177,29 +131,297 @@
         mixed_ref[r] = sums[r].astype(mixed_ref.dtype)
 
 
-def backward_kernel(grad_ref, padded_ref, taps_ref, cotan_ref, image_grad_ref, taps_grad_ref):
-    height = cotan_ref.shape[0]
-    taps = taps_ref[...]
-    lane = lax.broadcasted_iota(jnp.int32, taps.shape, 1)
-    taps_grad = jnp.zeros_like(taps)
-    sums = [None] * height
-    for v in range(KSIZE):
-        lines = [shifted(grad_ref[r], v - 3) for r in range(height + 6)]
-        for u in range(KSIZE):
-            t = u * KSIZE + v
-            tap = jnp.broadcast_to(taps[:, t : t + 1], lines[0].shape)
-            for r in range(height):
-                term = tap * lines[r + 6 - u]
-                sums[r] = term if sums[r] is None else sums[r] + term
-            both = [lines[r + 3] * padded_ref[r + u] for r in range(height)]
-            while len(both) > 1:
-                both = [p + q for p, q in zip(both[::2], both[1::2])] + both[len(both) // 2 * 2 :]
-            taps_grad = jnp.where(lane == t, jnp.sum(both[0], axis=1, keepdims=True), taps_grad)
-    for r in range(height):
-        image_grad_ref[r] = (sums[r] + cotan_ref[r].astype(jnp.float32)).astype(
-            image_grad_ref.dtype
+def flipped(index, bit):
+    return index + bit - 2 * bit * lax.rem(lax.div(index, bit), 2)
+
+
+def finish_kernel(
+    n,
+    rows,
+    part,
+    branch_ref,
+    normed_ref,
+    stats_ref,
+    sent_ref,
+    kept_ref,
+    mixed_ref,
+    padded_ref,
+    image_ref,
+    cotan_ref,
+    taps_ref,
+    gain_ref,
+    scale_ref,
+    block_ref,
+    image_grad_ref,
+    small_ref,
+    grads_ref,
+    branch_in,
+    normed_in,
+    stats_in,
+    core_in,
+    near_out,
+    near_in,
+    row_out,
+    row_in,
+    grad_pad,
+    running,
+    sums_one,
+    sums_two,
+    halo_out,
+    halo_in,
+    small_out,
+    small_in,
+    local_sem,
+    send_sem,
+    recv_sem,
+    pair_send,
+    pair_recv,
+):
+    f32, bf16 = jnp.float32, jnp.bfloat16
+    me = lax.axis_index("chan")
+    row = lax.axis_index("rows")
+    plane = lax.div(me, GROUP)
+    lines = pl.ds(lax.rem(me, GROUP) * part, part)
+    height, channels, breadth = mixed_ref.shape
+    planes = n // GROUP
+    steps = row_out.shape[0]
+    hidden = grads_ref.shape[1]
+    up, down = lax.rem(row + rows - 1, rows), lax.rem(row + 1, rows)
+    partners = [flipped(row, 2**s) for s in range(steps)]
+
+    barrier = pltpu.get_barrier_semaphore()
+    for k in range(1, n):
+        pl.semaphore_signal(
+            barrier, inc=1, device_id={"chan": lax.rem(me + k, n)}, device_id_type=MESH
         )
-    taps_grad_ref[...] = taps_grad
+    for other in [up, down] + partners:
+        pl.semaphore_signal(barrier, inc=1, device_id={"rows": other}, device_id_type=MESH)
+    pl.semaphore_wait(barrier, n + 1 + steps)
+
+    def pair(index, source, target, device):
+        copy = pltpu.make_async_remote_copy(
+            src_ref=source,
+            dst_ref=target,
+            send_sem=pair_send.at[index],
+            recv_sem=pair_recv.at[index],
+            device_id=device,
+            device_id_type=MESH,
+        )
+        copy.start()
+        return copy
+
+    def scatter(a, piece, target):
+        copies = []
+        for k in range(1, n):
+            peer = lax.rem(me + k, n)
+            copy = pltpu.make_async_remote_copy(
+                src_ref=piece(peer),
+                dst_ref=target.at[plane, lines],
+                send_sem=send_sem.at[a, k],
+                recv_sem=recv_sem.at[a, k],
+                device_id={"chan": peer},
+                device_id_type=MESH,
+            )
+            copy.start()
+            copies.append(copy)
+        copy = pltpu.make_async_copy(piece(me), target.at[plane, lines], local_sem.at[a])
+        copy.start()
+        return copies + [copy]
+
+    first = scatter(0, lambda peer: stats_ref, stats_in)
+    first += scatter(1, lambda peer: normed_ref.at[:, peer], normed_in)
+    core = pair(0, sent_ref, core_in, {"chan": flipped(me, 1)})
+    core.wait()
+
+    @pl.loop(0, hidden // 16)
+    def _(i):
+        for a in range(2):
+            own = pl.ds(pl.multiple_of(16 * i, 16), 16)
+            other = pl.ds(pl.multiple_of(hidden + 16 * i, 16), 16)
+            grads_ref[a, own, :] = kept_ref[a, own, :] + core_in[a, own, :].astype(f32)
+            near_out[a, own, :] = (
+                kept_ref[a, other, :] + core_in[a, other, :].astype(f32)
+            ).astype(bf16)
+
+    near = pair(1, near_out, near_in, {"chan": flipped(me, 2)})
+    for copy in first:
+        copy.wait()
+    last = scatter(2, lambda peer: branch_ref.at[:, peer], branch_in)
+
+    sums_one[...] = jnp.zeros_like(sums_one)
+    sums_two[...] = jnp.zeros_like(sums_two)
+
+    def normalize(start, stop):
+        @pl.loop(start, stop)
+        def _(r):
+            grad_normed = normed_in[0, r].astype(f32)
+            stats = stats_in[0, r]
+            centre, inv_scale = stats[2:3], stats[3:4]
+            for p in range(1, planes):
+                grad_normed += normed_in[p, r].astype(f32)
+                stats += stats_in[p, r]
+            unit = (mixed_ref[r].astype(f32) - centre) * inv_scale
+            sums_one[...] += grad_normed * unit
+            scaled_grad = grad_normed * gain_ref[...]
+            mixed_grad = inv_scale * (
+                scaled_grad - stats[0:1] * (1.0 / D) - unit * (stats[1:2] * (1.0 / D))
+            )
+            grad_pad[r + 3] = mixed_grad.astype(bf16).astype(f32)
+
+    normalize(0, 3)
+    normalize(height - 3, height)
+    for i in range(3):
+        halo_out[0, i] = grad_pad[3 + i].astype(bf16)
+        halo_out[1, i] = grad_pad[height + i].astype(bf16)
+    halos = [
+        pair(2, halo_out.at[0], halo_in.at[1], {"rows": up}),
+        pair(3, halo_out.at[1], halo_in.at[0], {"rows": down}),
+    ]
+    normalize(3, height - 3)
+    near.wait()
+
+    @pl.loop(0, hidden // 16)
+    def _(i):
+        for a in range(2):
+            own = pl.ds(pl.multiple_of(16 * i, 16), 16)
+            row_out[0, a, own, :] = (grads_ref[a, own, :] + near_in[a, own, :].astype(f32)).astype(
+                bf16
+            )
+
+    step = pair(4, row_out.at[0], row_in.at[0], {"rows": partners[0]})
+    for copy in halos:
+        copy.wait()
+    above = jnp.where(row > 0, 1.0, 0.0).astype(f32)
+    below = jnp.where(row < rows - 1, 1.0, 0.0).astype(f32)
+    for i in range(3):
+        grad_pad[i] = halo_in[0, i].astype(f32) * above
+        grad_pad[height + 3 + i] = halo_in[1, i].astype(f32) * below
+
+    @pl.loop(0, channels // 8)
+    def _(g):
+        group = pl.ds(pl.multiple_of(8 * g, 8), 8)
+        taps = taps_ref[group, :]
+        lane = lax.broadcasted_iota(jnp.int32, taps.shape, 1)
+        taps_grad = jnp.zeros_like(taps)
+        sums = [None] * height
+        for v in range(KSIZE):
+            shifts = [shifted(grad_pad[r, group, :], v - 3) for r in range(height + 6)]
+            for u in range(KSIZE):
+                t = u * KSIZE + v
+                tap = jnp.broadcast_to(taps[:, t : t + 1], taps.shape)
+                for r in range(height):
+                    term = tap * shifts[r + 6 - u]
+                    sums[r] = term if sums[r] is None else sums[r] + term
+                both = [shifts[r + 3] * padded_ref[r + u, group, :] for r in range(height)]
+                while len(both) > 1:
+                    both = [p + q for p, q in zip(both[::2], both[1::2])] + both[
+                        len(both) // 2 * 2 :
+                    ]
+                taps_grad = jnp.where(
+                    lane == t, jnp.sum(both[0], axis=1, keepdims=True), taps_grad
+                )
+        for r in range(height):
+            running[r, group, :] = sums[r]
+        small_ref[group, :] = taps_grad
+
+    @pl.loop(0, height)
+    def _(r):
+        image_grad_ref[r] = (running[r] + cotan_ref[r].astype(f32)).astype(bf16)
+
+    for s in range(steps):
+        step.wait()
+        final = s == steps - 1
+
+        @pl.loop(0, hidden // 16)
+        def _(i):
+            for a in range(2):
+                own = pl.ds(pl.multiple_of(16 * i, 16), 16)
+                total = row_out[s, a, own, :].astype(f32) + row_in[s, a, own, :].astype(f32)
+                if final:
+                    grads_ref[a, own, :] = total
+                else:
+                    row_out[s + 1, a, own, :] = total.astype(bf16)
+
+        if not final:
+            step = pair(
+                5 + s, row_out.at[s + 1], row_in.at[s + 1], {"rows": partners[s + 1]}
+            )
+    for copy in last:
+        copy.wait()
+
+    @pl.loop(0, height)
+    def _(r):
+        branch = branch_in[0, r].astype(f32)
+        for p in range(1, planes):
+            branch += branch_in[p, r].astype(f32)
+        sums_two[...] += branch * cotan_ref[r].astype(f32)
+        block_ref[r] = (image_ref[r].astype(f32) + scale_ref[...] * branch).astype(bf16)
+
+    lane = lax.broadcasted_iota(jnp.int32, small_ref.shape, 1)
+    small = small_ref[...]
+    small = jnp.where(lane == KSIZE * KSIZE, jnp.sum(sums_one[...], axis=1, keepdims=True), small)
+    small = jnp.where(
+        lane == KSIZE * KSIZE + 1, jnp.sum(sums_two[...], axis=1, keepdims=True), small
+    )
+    for s in range(steps):
+        small_out[s] = small
+        step = pair(4 + steps + s, small_out.at[s], small_in.at[s], {"rows": partners[s]})
+        step.wait()
+        small = small + small_in[s]
+    small_ref[...] = small
+
+
+def finish(n, part, arrays, hidden):
+    f32, bf16 = jnp.float32, jnp.bfloat16
+    height, channels, breadth = arrays[5].shape
+    width = arrays[3].shape[2]
+    planes = n // GROUP
+    rows = lax.axis_size("rows")
+    steps = rows.bit_length() - 1
+    pairs = 4 + 2 * steps
+    vmem = pl.BlockSpec(memory_space=pltpu.VMEM)
+    hbm = pl.BlockSpec(memory_space=pl.ANY)
+    dma = pltpu.SemaphoreType.DMA
+    return pl.pallas_call(
+        functools.partial(finish_kernel, n, rows, part),
+        out_shape=(
+            jax.ShapeDtypeStruct((height, channels, breadth), bf16),
+            jax.ShapeDtypeStruct((height, channels, breadth), bf16),
+            jax.ShapeDtypeStruct((channels, 128), f32),
+            jax.ShapeDtypeStruct((2, hidden, width), f32),
+        ),
+        in_specs=[hbm] * 4 + [vmem] * 8,
+        out_specs=(vmem, vmem, vmem, vmem),
+        scratch_shapes=[
+            pltpu.VMEM((planes, height, channels, breadth), bf16),
+            pltpu.VMEM((planes, height, channels, breadth), bf16),
+            pltpu.VMEM((planes, height, 4, breadth), f32),
+            pltpu.VMEM((2, 2 * hidden, width), bf16),
+            pltpu.VMEM((2, hidden, width), bf16),
+            pltpu.VMEM((2, hidden, width), bf16),
+            pltpu.VMEM((steps, 2, hidden, width), bf16),
+            pltpu.VMEM((steps, 2, hidden, width), bf16),
+            pltpu.VMEM((height + 6, channels, breadth), f32),
+            pltpu.VMEM((height, channels, breadth), f32),
+            pltpu.VMEM((channels, breadth), f32),
+            pltpu.VMEM((channels, breadth), f32),
+            pltpu.VMEM((2, 3, channels, breadth), bf16),
+            pltpu.VMEM((2, 3, channels, breadth), bf16),
+            pltpu.VMEM((steps, channels, 128), f32),
+            pltpu.VMEM((steps, channels, 128), f32),
+            dma((3,)),
+            dma((3, n)),
+            dma((3, n)),
+            dma((pairs,)),
+            dma((pairs,)),
+        ],
+        compiler_params=pltpu.CompilerParams(
+            collective_id=1, has_side_effects=True, vmem_limit_bytes=36 * 2**20
+        ),
+        cost_estimate=pl.CostEstimate(
+            flops=40000000, bytes_accessed=100000000, transcendentals=0
+        ),
+    )(*arrays)
 
 
 def stencil(kernel, arrays, outs):
@@ -283,54 +505,32 @@
     stats = jnp.transpose(stats.reshape(4, part, breadth), (1, 0, 2))
     grad_w_in = lax.dot_general(grad_pre, normed, contract_tail, preferred_element_type=f32)
     grad_w_out = lax.dot_general(activated, scaled_all, contract_tail, preferred_element_type=f32)
-    branch_all, normed_all, stats_all = exchange(
-        collect_kernel,
-        1,
-        (split(branch_part), split(normed_part.astype(bf16)), stats),
-        (
-            (planes, height, channels, breadth),
-            (planes, height, channels, breadth),
-            (planes, height, 4, breadth),
-        ),
+    half = grad_w_in.shape[0] // 2
+    sent = jnp.stack([grad_w_in[half:].astype(bf16), grad_w_out[half:].astype(bf16)])
+    kept = jnp.stack([grad_w_in[:half], grad_w_out[:half]])
+    block_out, image_grad, small, grads = finish(
         n,
         part,
-    )
-    grads = jnp.stack([grad_w_in, grad_w_out])
-    for bit in (1, 2):
-        half = grads.shape[1] // 2
-        grads = grads[:, :half] + swap(grads[:, half:].astype(bf16), "chan", bit).astype(f32)
-    grads = total_over(grads, "rows")
-    branch = jnp.sum(branch_all.astype(f32), axis=0)
-    grad_normed = jnp.sum(normed_all.astype(f32), axis=0)
-    total_one = jnp.sum(stats_all[:, :, 0:1], axis=0)
-    total_two = jnp.sum(stats_all[:, :, 1:2], axis=0)
-    centre, inv_scale = stats_all[0, :, 2:3], stats_all[0, :, 3:4]
-    unit_norm = (mixed_in.astype(f32) - centre) * inv_scale
-    scaled_grad = grad_normed * ln_gain[:, None]
-    grad_mixed = (inv_scale * (scaled_grad - total_one / D - unit_norm * (total_two / D))).astype(
-        bf16
-    )
-    rimmed_grad = extended(grad_mixed, "rows").astype(f32)
-    image_grad, grad_kernel = stencil(
-        backward_kernel,
-        (rimmed_grad, padded, taps, cotan_rows),
         (
-            jax.ShapeDtypeStruct(image_rows.shape, bf16),
-            jax.ShapeDtypeStruct((channels, 128), f32),
-        ),
-    )
-    block_out = (image_rows.astype(f32) + layer_scale[:, None] * branch).astype(bf16)
-    grad_scale = jnp.sum(cotan_rows.astype(f32) * branch, axis=(0, 2))
-    grad_gain = jnp.sum(grad_normed * unit_norm, axis=(0, 2))
-    small = jnp.concatenate(
-        [grad_kernel[:, : KSIZE * KSIZE], grad_gain[:, None], grad_scale[:, None]], axis=1
-    )
-    small = total_over(small, "rows")
-    grad_kernel = small[:, : KSIZE * KSIZE].reshape(channels, KSIZE, KSIZE)
+            split(branch_part),
+            split(normed_part.astype(bf16)),
+            stats,
+            sent,
+            kept,
+            mixed_in,
+            padded,
+            image_rows,
+            cotan_rows,
+            taps,
+            jnp.broadcast_to(ln_gain[:, None], (channels, breadth)),
+            jnp.broadcast_to(layer_scale[:, None], (channels, breadth)),
+        ),
+        half // 2,
+    )
     return (
         jnp.transpose(block_out, (1, 0, 2))[:, None],
         jnp.transpose(image_grad, (1, 0, 2))[:, None],
-        grad_kernel,
+        small[:, : KSIZE * KSIZE].reshape(channels, KSIZE, KSIZE),
         small[:, KSIZE * KSIZE],
         small[:, KSIZE * KSIZE + 1],
         grads[0].T,

time: 170 us -> 135 us (0.79)
  the two profiles are of different devices: /device:TPU:12 before, /device:TPU:0 now
where the time goes in v3:
time: 135 us
  Pallas kernels  96.8 us (72%)
  local copies, waits for them, and re-layouts  9.96 us (7%)
  matrix products  8.58 us (6%)
  starting transfers between devices  7.79 us (6%)
  waiting for transfers between devices  5.52 us (4%)
  other arithmetic  5.25 us (4%)
    pallas_call x1, Pallas kernels, finish(): pl.pallas_call(functools.partial(finish_kernel, n, rows, part), out_shape...  59.8 us
    pallas_call x1, Pallas kernels, exchange(): pl.pallas_call(functools.partial(kernel, n, part), out_shape=tuple((jax.S...  32.1 us
    ppermute x2, waiting for transfers between devices, swap(): return lax.ppermute(value, axis, [(i, i ^ bit) for i in range(n)])  5.51 us
    pallas_call x1, Pallas kernels, stencil(): pl.pallas_call(kernel, grid=(channels // 8,), out_shape=tuple(outs), in_s...  5 us
    dot_general x1, matrix products, body(): pre_act = jnp.dot(weights[0], normed, preferred_element_type=f32)  3.99 us
    ppermute x1, starting transfers between devices, extended(): low = lax.ppermute(block[-3:], axis, forward)  3.43 us
    unnamed x22, local copies, waits for them, and re-layouts  3.2 us
    ppermute x2, starting transfers between devices, swap(): return lax.ppermute(value, axis, [(i, i ^ bit) for i in range(n)])  3.08 us
  transfers between devices with their start and end apart: 4, of which 1 were waited for; matrix products, arithmetic and copies ran while one was open for 5% of the time, Pallas kernels for 27%

profile of v3, /device:TPU:0, one launch (start us, length us, event | category | flops | bytes accessed | tf_op | source)
XLA Modules:
  0.0 134.9 jit_solution(15912883162452722598)
XLA Ops:
  0.6 0.0 copy-start.3
  0.6 0.0 copy-start.4
  0.7 0.0 copy-start.6
  0.7 0.0 copy-start.8
  0.7 0.0 copy-start.5
  0.7 0.0 copy-start.7
  0.7 1.2 pad_maximum_fusion.8
  1.9 3.0 %collective-permute-start = (bf16[2,192,768]{2,1,0:T(8,128)(2,1)S(1)}, bf16[2,192,768]{2,1,0:T(8,128)(2,1)S(1)}, u32[]{:S(2)}, u32[]{:S(2)}) collective-permute-start(bf16[2,192,768]{2,1,0:T(8,128)(2,1)S(1)} %pad_maximum_fusion.8), channel_id=1, source_target_pairs={{0,4},{2,6},{4,0},{6,2},{8,12},{10,14},{12,8},{14,10},{16,20},{18,... | collective-permute-start | bytes 1769480 | tf_op jit(solution)/shard_map/ppermute | solution.py:105
  4.9 1.0 copy.31
  5.9 3.4 %collective-permute-start.2 = (bf16[3,48,128]{2,1,0:T(8,128)(2,1)S(1)}, bf16[3,48,128]{2,1,0:T(8,128)(2,1)S(1)}, u32[]{:S(2)}, u32[]{:S(2)}) collective-permute-start(bf16[3,48,128]{2,1,0:T(8,128)(2,1)S(1)} %get-tuple-element.58), channel_id=1, source_target_pairs={{0,1},{2,3},{4,5},{6,7},{8,9},{10,11},{12,13},{14,15},{16,17},{18,... | collective-permute-start | bytes 110600 | tf_op jit(solution)/shard_map/ppermute | solution.py:23
  9.3 1.3 collective-permute-start.3
  10.6 0.0 copy-done.6
  10.6 0.1 copy.21
  10.7 0.0 copy-done.8
  10.7 0.5 pad.9.refs_2_
  11.2 0.6 pad.8.taps_ref
  11.8 0.1 copy.30
  11.9 0.8 multiply_convert_fusion.refs_1_
  12.7 5.5 %collective-permute-done = bf16[2,192,768]{2,1,0:T(8,128)(2,1)S(1)} collective-permute-done((bf16[2,192,768]{2,1,0:T(8,128)(2,1)S(1)}, bf16[2,192,768]{2,1,0:T(8,128)(2,1)S(1)}, u32[]{:S(2)}, u32[]{:S(2)}) %collective-permute-start) | collective-permute-done | bytes 589856 | tf_op jit(solution)/shard_map/ppermute | solution.py:105
  18.2 0.1 pad_maximum_fusion.2
  18.3 0.1 collective-permute-start.1
  18.4 0.0 collective-permute-done.2
  18.4 0.0 collective-permute-done.3
  18.4 0.8 maximum_convert_fusion.padded_ref
  19.2 5.0 %shard_map.126.refs_0_.mixed_ref = bf16[16,48,128]{2,1,0:T(8,128)(2,1)} custom-call(f32[22,48,128]{2,1,0:T(8,128)} %maximum_convert_fusion.padded_ref, f32[48,128]{1,0:T(8,128)} %pad.8.taps_ref), custom_call_target="tpu_custom_call" | custom-call | flops 10000000 | bytes 6000000 | tf_op jit(solution)/shard_map/pallas_call | solution.py:435
  24.2 32.1 %shard_map.127 = (bf16[4,16,48,128]{3,2,1,0:T(8,128)(2,1)}, bf16[4,16,48,128]{3,2,1,0:T(8,128)(2,1)}, f32[1,16,1,128]{3,2,1,0:T(1,128)}) custom-call(bf16[16,48,128]{2,1,0:T(8,128)(2,1)} %shard_map.126.refs_0_.mixed_ref, bf16[16,48,128]{2,1,0:T(8,128)(2,1)} %multiply_convert_fusion.refs_1_, f32[1,1,128]{2,1,0:T(1,128)} %pad.9.refs_2_), custom_call_target="tpu_custom_call" | custom-call | bytes 39372800 | tf_op jit(solution)/shard_map/pallas_call | solution.py:86
  56.3 0.7 slice_reduce_fusion.2
  57.0 0.1 mul.75
  57.1 1.6 %fusion.34 = (bf16[1,16,48,128]{3,2,1,0:T(8,128)(2,1)S(1)}, bf16[1,16,48,128]{3,2,1,0:T(8,128)(2,1)S(1)}, bf16[1,16,48,128]{3,2,1,0:T(8,128)(2,1)S(1)}, bf16[1,1...) fusion(bf16[4,16,48,128]{3,2,1,0:T(8,128)(2,1)} %get-tuple-elem, ...), kind=kLoop, calls=%fused_computation.73 | loop fusion | bytes 3145728 | tf_op jit(solution)/shard_map/slice | solution.py:479
  58.7 0.2 convert_reduce_fusion
  58.9 0.3 fusion.6
  59.1 0.0 collective-permute-done.1
  59.1 1.4 %pad_maximum_fusion = bf16[2,768,768]{2,1,0:T(8,128)(2,1)S(1)} fusion(bf16[2,384,768]{2,1,0:T(8,128)(2,1)} %collective-permute-done.1, bf16[2,192,768]{2,1,0:T(8,128)(2,1)S(1)} %collective-permute-done, bf16[1,192,768]{2,1,0:T(8,128)(2,1)S(1)} %bitcast.89, bf16[1,192,768]{2,1,0:T(8,128)(2,1)S(1)} %bitcast.92), kind=kLoop, calls=%fused_computation.2 | loop fusion | flops 9437184 | bytes 4718592 | tf_op jit(solution)/shard_map/concatenate | solution.py:462
  60.6 4.0 %fusion.9 = (bf16[768,512]{1,0:T(8,128)(2,1)S(1)}, f32[768,512]{1,0:T(8,128)S(1)}) fusion(f32[768]{0:T(1024)S(1)} %mul.75, f32[512]{0:T(512)S(1)} %add_rsqrt_fusion, f32[512]{0:T(512)S(1)} %broadcast_multiply_fusion, bf16[768,128]{1,0:T(8,128)(2,1)S(1)} %bitcast.105, bf16[768,128]{1,0:T(8,128)(2,1)S(1)} %bitcast.100, bf16[768,128]{1,0:T(8,128)(2,1)S(1)} %bitcast.95, ...), kind=kOutput, calls=%fused_computation.15 | convolution fusion | flops 634257408 | bytes 4333568 | tf_op jit(solution)/shard_map/dot_general | solution.py:493
  64.6 1.1 fusion.15
  65.7 1.0 multiply_reduce_fusion
  66.7 0.9 fusion.28
  67.6 0.1 fusion.25
  67.6 0.1 slice_bitcast_fusion.1
  67.7 0.8 convolution_convert_fusion
  68.5 0.8 fusion.27
  69.3 0.1 fusion.26
  69.4 0.1 slice_bitcast_fusion
  69.5 0.1 fusion.35
  69.6 0.1 fusion.33
  69.8 0.2 pad_maximum_fusion.1.kept_ref
  70.0 0.1 pad_maximum_fusion.3.sent_ref
  70.1 0.0 copy-start
  70.1 0.0 copy-start.1
  70.1 0.0 copy-start.2
  70.1 0.1 pad_maximum_fusion.5.branch_ref
  70.2 0.1 pad_maximum_fusion.7.normed_ref
  70.4 0.1 broadcast_in_dim.11.gain_ref
  70.4 0.1 broadcast_in_dim.12.scale_ref
  70.5 0.6 copy-done
  71.1 0.0 copy-done.1
  71.2 0.0 copy-done.2
  71.2 59.8 %shard_map.128 = (bf16[16,48,128]{2,1,0:T(8,128)(2,1)S(1)}, bf16[16,48,128]{2,1,0:T(8,128)(2,1)S(1)}, f32[48,128]{1,0:T(8,128)S(1)}, f32[2,192,768]{2,1,0:T(8,128)S(1)}) custom-call(bf16[4,16,48,128]{3,2,1,0:T(8,128)(2,1)S(1)} %pad_maximum_fusion.5.branch_ref, bf16[4,16,48,128]{3,2,1,0:T(8,128)(2,1)S(1)} %pad_maximum_fusion.7.normed_ref, ...), custom_call_target="tpu_custom_call" | custom-call | flops 40000000 | bytes 100000000 | tf_op jit(solution)/shard_map/pallas_call | solution.py:385
  131.0 0.7 copy.24
  131.7 0.7 copy.25
  132.4 0.7 slice_reduce_fusion
  133.1 0.1 copy.23
  133.2 0.6 reshape.109
  133.8 1.1 slice_bitcast_fusion.8
  (9 shorter events, 0.0 us)
Async XLA Ops:
  0.6 17.6 %copy-start.3 = (bf16[192,768]{1,0:T(8,128)(2,1)S(1)}, bf16[192,768]{1,0:T(8,128)(2,1)}, u32[]{:S(2)}) copy-start(bf16[192,768]{1,0:T(8,128)(2,1)} %param.11) | copy-start | bytes 884740
  0.6 17.6 %copy-start.4 = (bf16[768,192]{0,1:T(8,128)(2,1)S(1)}, bf16[768,192]{0,1:T(8,128)(2,1)}, u32[]{:S(2)}) copy-start(bf16[768,192]{0,1:T(8,128)(2,1)} %param.10) | copy-start | bytes 884740
  0.7 9.9 %copy-start.6 = (f32[48,7,7]{0,2,1:T(8,128)S(1)}, f32[48,7,7]{0,2,1:T(8,128)}, u32[]{:S(2)}) copy-start(f32[48,7,7]{0,2,1:T(8,128)} %param.8) | copy-start | bytes 28228
  0.7 10.0 %copy-start.8 = (f32[48]{0:T(128)S(1)}, f32[48]{0:T(128)}, u32[]{:S(2)}) copy-start(f32[48]{0:T(128)} %param.9) | copy-start | bytes 580
  0.7 11.2 %copy-start.5 = (bf16[48,1,16,128]{3,2,1,0:T(8,128)(2,1)S(1)}, bf16[48,1,16,128]{3,2,1,0:T(8,128)(2,1)}, u32[]{:S(2)}) copy-start(bf16[48,1,16,128]{3,2,1,0:T(8,128)(2,1)} %param.13) | copy-start | bytes 589828
  0.7 11.2 %copy-start.7 = (f32[48]{0:T(128)S(1)}, f32[48]{0:T(128)}, u32[]{:S(2)}) copy-start(f32[48]{0:T(128)} %param.12) | copy-start | bytes 580
  1.9 16.3 %collective-permute-start = (bf16[2,192,768]{2,1,0:T(8,128)(2,1)S(1)}, bf16[2,192,768]{2,1,0:T(8,128)(2,1)S(1)}, u32[]{:S(2)}, u32[]{:S(2)}) collective-permute-start(bf16[2,192,768]{2,1,0:T(8,128)(2,1)S(1)} %pad_maximum_fusion.8), channel_id=1, source_target_pairs={{0,4},{2,6},{4,0},{6,2},{8,12},{10,14},{12,8},{14,10},{16,20},{18,... | collective-permute-start | bytes 1769480 | tf_op jit(solution)/shard_map/ppermute | solution.py:105
  5.9 12.5 %collective-permute-start.2 = (bf16[3,48,128]{2,1,0:T(8,128)(2,1)S(1)}, bf16[3,48,128]{2,1,0:T(8,128)(2,1)S(1)}, u32[]{:S(2)}, u32[]{:S(2)}) collective-permute-start(bf16[3,48,128]{2,1,0:T(8,128)(2,1)S(1)} %get-tuple-element.58), channel_id=1, source_target_pairs={{0,1},{2,3},{4,5},{6,7},{8,9},{10,11},{12,13},{14,15},{16,17},{18,... | collective-permute-start | bytes 110600 | tf_op jit(solution)/shard_map/ppermute | solution.py:23
  9.3 9.1 %collective-permute-start.3 = (bf16[3,48,128]{2,1,0:T(8,128)(2,1)S(1)}, bf16[3,48,128]{2,1,0:T(8,128)(2,1)S(1)}, u32[]{:S(2)}, u32[]{:S(2)}) collective-permute-start(bf16[3,48,128]{2,1,0:T(8,128)(2,1)S(1)} %get-tuple-element.59), channel_id=1, source_target_pairs={{1,0},{3,2},{5,4},{7,6},{9,8},{11,10},{13,12},{15,14},{17,16},{19,... | collective-permute-start | bytes 110600 | tf_op jit(solution)/shard_map/ppermute | solution.py:24
  18.3 40.9 %collective-permute-start.1 = (bf16[2,384,768]{2,1,0:T(8,128)(2,1)S(1)}, bf16[2,384,768]{2,1,0:T(8,128)(2,1)}, u32[]{:S(2)}, u32[]{:S(2)}) collective-permute-start(bf16[2,384,768]{2,1,0:T(8,128)(2,1)S(1)} %pad_maximum_fusion.2), channel_id=1, source_target_pairs={{0,2},{2,0},{4,6},{6,4},{8,10},{10,8},{12,14},{14,12},{16,18},{18,... | collective-permute-start | bytes 3538952 | tf_op jit(solution)/shard_map/ppermute | solution.py:105
  70.1 1.1 copy-start
  70.1 1.1 copy-start.1
  70.1 1.1 copy-start.2

commit v4 on v3

--- a/solution.py
+++ b/solution.py
@@ -16,15 +16,6 @@
 inv_root_two_pi = 0.3989422804014327
 
 
-def extended(block, axis):
-    count = lax.axis_size(axis)
-    forward = [(i, i + 1) for i in range(count - 1)]
-    backward = [(target, source) for source, target in forward]
-    low = lax.ppermute(block[-3:], axis, forward)
-    high = lax.ppermute(block[:3], axis, backward)
-    return jnp.concatenate([low, block, high], axis=0)
-
-
 def gelu_slope(values):
     return (
         0.5 * (1.0 + lax.erf(values * inv_root_two))
@@ -34,75 +25,6 @@
 
 GROUP = 4
 MESH = pl.DeviceIdType.MESH
-
-
-def greet(n, me):
-    barrier = pltpu.get_barrier_semaphore()
-    for k in range(1, n):
-        pl.semaphore_signal(
-            barrier, inc=1, device_id={"chan": lax.rem(me + k, n)}, device_id_type=MESH
-        )
-    pl.semaphore_wait(barrier, n - 1)
-
-
-def spread_kernel(n, part, *refs):
-    count = (len(refs) - 3) // 2
-    sources, targets = refs[:count], refs[count : 2 * count]
-    local_sem, send_sem, recv_sem = refs[2 * count :]
-    me = lax.axis_index("chan")
-    greet(n, me)
-
-    def piece(ref, peer):
-        if ref.shape[0] == part * GROUP:
-            return ref.at[pl.ds(lax.rem(peer, GROUP) * part, part)]
-        return ref
-
-    copies = []
-    for k in range(1, n):
-        peer = lax.rem(me + k, n)
-        for a in range(count):
-            copy = pltpu.make_async_remote_copy(
-                src_ref=piece(sources[a], peer),
-                dst_ref=targets[a].at[:, me],
-                send_sem=send_sem.at[a, k],
-                recv_sem=recv_sem.at[a, k],
-                device_id={"chan": peer},
-                device_id_type=MESH,
-            )
-            copy.start()
-            copies.append(copy)
-    own = []
-    for a in range(count):
-        copy = pltpu.make_async_copy(piece(sources[a], me), targets[a].at[:, me], local_sem.at[a])
-        copy.start()
-        own.append(copy)
-    for copy in own + copies:
-        copy.wait()
-
-
-def exchange(kernel, identity, arrays, shapes, n, part):
-    count = len(arrays)
-    size = sum(a.size * a.dtype.itemsize for a in arrays)
-    return pl.pallas_call(
-        functools.partial(kernel, n, part),
-        out_shape=tuple(
-            jax.ShapeDtypeStruct(shape, a.dtype) for shape, a in zip(shapes, arrays)
-        ),
-        in_specs=[pl.BlockSpec(memory_space=pl.ANY)] * count,
-        out_specs=tuple([pl.BlockSpec(memory_space=pl.ANY)] * count),
-        scratch_shapes=[
-            pltpu.SemaphoreType.DMA((count,)),
-            pltpu.SemaphoreType.DMA((count, n)),
-            pltpu.SemaphoreType.DMA((count, n)),
-        ],
-        compiler_params=pltpu.CompilerParams(collective_id=identity, has_side_effects=True),
-        cost_estimate=pl.CostEstimate(flops=0, bytes_accessed=100 * size, transcendentals=0),
-    )(*arrays)
-
-
-def swap(value, axis, bit):
-    n = lax.axis_size(axis)
-    return lax.ppermute(value, axis, [(i, i ^ bit) for i in range(n)])
 
 
 def shifted(value, shift):
@@ -113,22 +35,6 @@
     rolled = pltpu.roll(value, shift % breadth, 1)
     keep = lane >= shift if shift > 0 else lane < breadth + shift
     return jnp.where(keep, rolled, 0.0)
-
-
-def forward_kernel(padded_ref, taps_ref, mixed_ref):
-    height = mixed_ref.shape[0]
-    taps = taps_ref[...]
-    sums = [None] * height
-    for v in range(KSIZE):
-        lines = [shifted(padded_ref[r], 3 - v) for r in range(height + 6)]
-        for u in range(KSIZE):
-            t = u * KSIZE + v
-            tap = jnp.broadcast_to(taps[:, t : t + 1], lines[0].shape)
-            for r in range(height):
-                term = tap * lines[r + u]
-                sums[r] = term if sums[r] is None else sums[r] + term
-    for r in range(height):
-        mixed_ref[r] = sums[r].astype(mixed_ref.dtype)
 
 
 def flipped(index, bit):
@@ -424,22 +330,163 @@
     )(*arrays)
 
 
-def stencil(kernel, arrays, outs):
-    channels = arrays[0].shape[1]
-
-    def spec(value):
-        if len(value.shape) == 2:
-            return pl.BlockSpec((8, value.shape[1]), lambda i: (i, 0))
-        return pl.BlockSpec((value.shape[0], 8, value.shape[2]), lambda i: (0, i, 0))
-
+def lead_kernel(
+    n,
+    rows,
+    part,
+    image_ref,
+    taps_ref,
+    scaled_ref,
+    gain_ref,
+    weights_ref,
+    mixed_all,
+    scaled_all,
+    gain_all,
+    weights_all,
+    padded_ref,
+    mixed_ref,
+    running,
+    halo_in,
+    local_sem,
+    send_sem,
+    recv_sem,
+    pair_send,
+    pair_recv,
+):
+    f32, bf16 = jnp.float32, jnp.bfloat16
+    me = lax.axis_index("chan")
+    row = lax.axis_index("rows")
+    height, channels, breadth = image_ref.shape
+    hidden = weights_ref.shape[1]
+    up, down = lax.rem(row + rows - 1, rows), lax.rem(row + 1, rows)
+
+    barrier = pltpu.get_barrier_semaphore()
+    for k in range(1, n):
+        pl.semaphore_signal(
+            barrier, inc=1, device_id={"chan": lax.rem(me + k, n)}, device_id_type=MESH
+        )
+    for other in [up, down]:
+        pl.semaphore_signal(barrier, inc=1, device_id={"rows": other}, device_id_type=MESH)
+    pl.semaphore_wait(barrier, n + 1)
+
+    def pair(index, source, target, device):
+        copy = pltpu.make_async_remote_copy(
+            src_ref=source,
+            dst_ref=target,
+            send_sem=pair_send.at[index],
+            recv_sem=pair_recv.at[index],
+            device_id=device,
+            device_id_type=MESH,
+        )
+        copy.start()
+        return copy
+
+    def scatter(a, piece, target):
+        copies = []
+        for k in range(1, n):
+            peer = lax.rem(me + k, n)
+            copy = pltpu.make_async_remote_copy(
+                src_ref=piece(peer),
+                dst_ref=target.at[:, me],
+                send_sem=send_sem.at[a, k],
+                recv_sem=recv_sem.at[a, k],
+                device_id={"chan": peer},
+                device_id_type=MESH,
+            )
+            copy.start()
+            copies.append(copy)
+        copy = pltpu.make_async_copy(piece(me), target.at[:, me], local_sem.at[a])
+        copy.start()
+        return copies + [copy]
+
+    def lines(peer):
+        return pl.ds(lax.rem(peer, GROUP) * part, part)
+
+    def block(index):
+        return weights_all.at[:, pl.ds(index * hidden, hidden)]
+
+    halos = [
+        pair(0, image_ref.at[pl.ds(0, 3)], halo_in.at[1], {"rows": up}),
+        pair(1, image_ref.at[pl.ds(height - 3, 3)], halo_in.at[0], {"rows": down}),
+    ]
+    near = pair(2, weights_ref, block(1), {"chan": flipped(me, 2)})
+    core = pair(3, weights_ref, block(2), {"chan": flipped(me, 1)})
+    own = pltpu.make_async_copy(weights_ref, block(0), local_sem.at[3])
+    own.start()
+    copies = scatter(0, lambda peer: scaled_ref.at[lines(peer)], scaled_all)
+    copies += scatter(1, lambda peer: gain_ref, gain_all)
+
+    @pl.loop(0, height)
+    def _(r):
+        padded_ref[r + 3] = image_ref[r].astype(f32)
+
+    for copy in halos:
+        copy.wait()
+    above = jnp.where(row > 0, 1.0, 0.0).astype(f32)
+    below = jnp.where(row < rows - 1, 1.0, 0.0).astype(f32)
+    for i in range(3):
+        padded_ref[i] = halo_in[0, i].astype(f32) * above
+        padded_ref[height + 3 + i] = halo_in[1, i].astype(f32) * below
+
+    @pl.loop(0, channels // 8)
+    def _(g):
+        group = pl.ds(pl.multiple_of(8 * g, 8), 8)
+        taps = taps_ref[group, :]
+        sums = [None] * height
+        for v in range(KSIZE):
+            shifts = [shifted(padded_ref[r, group, :], 3 - v) for r in range(height + 6)]
+            for u in range(KSIZE):
+                t = u * KSIZE + v
+                tap = jnp.broadcast_to(taps[:, t : t + 1], taps.shape)
+                for r in range(height):
+                    term = tap * shifts[r + u]
+                    sums[r] = term if sums[r] is None else sums[r] + term
+        for r in range(height):
+            running[r, group, :] = sums[r]
+
+    @pl.loop(0, height)
+    def _(r):
+        mixed_ref[r] = running[r].astype(bf16)
+
+    copies += scatter(2, lambda peer: mixed_ref.at[lines(peer)], mixed_all)
+    near.wait()
+    far = pair(4, block(1), block(3), {"chan": flipped(me, 1)})
+    for copy in copies + [own, core, far]:
+        copy.wait()
+
+
+def lead(n, part, arrays):
+    f32, bf16 = jnp.float32, jnp.bfloat16
+    height, channels, breadth = arrays[0].shape
+    hidden, width = arrays[4].shape[1:]
+    rows = lax.axis_size("rows")
+    vmem = pl.BlockSpec(memory_space=pltpu.VMEM)
+    hbm = pl.BlockSpec(memory_space=pl.ANY)
+    dma = pltpu.SemaphoreType.DMA
     return pl.pallas_call(
-        kernel,
-        grid=(channels // 8,),
-        out_shape=tuple(outs),
-        in_specs=[spec(a) for a in arrays],
-        out_specs=tuple(spec(o) for o in outs),
+        functools.partial(lead_kernel, n, rows, part),
+        out_shape=(
+            jax.ShapeDtypeStruct((part, n, channels, breadth), bf16),
+            jax.ShapeDtypeStruct((part, n, channels, breadth), bf16),
+            jax.ShapeDtypeStruct((1, n, 1, 128), f32),
+            jax.ShapeDtypeStruct((2, GROUP * hidden, width), bf16),
+            jax.ShapeDtypeStruct((height + 6, channels, breadth), f32),
+            jax.ShapeDtypeStruct((height, channels, breadth), bf16),
+        ),
+        in_specs=[vmem, vmem, hbm, hbm, hbm],
+        out_specs=(hbm, hbm, hbm, hbm, vmem, vmem),
+        scratch_shapes=[
+            pltpu.VMEM((height, channels, breadth), f32),
+            pltpu.VMEM((2, 3, channels, breadth), bf16),
+            dma((4,)),
+            dma((3, n)),
+            dma((3, n)),
+            dma((5,)),
+            dma((5,)),
+        ],
+        compiler_params=pltpu.CompilerParams(collective_id=0, has_side_effects=True),
         cost_estimate=pl.CostEstimate(
-            flops=10000000, bytes_accessed=6000000, transcendentals=0
+            flops=20000000, bytes_accessed=100000000, transcendentals=0
         ),
     )(*arrays)
 
@@ -456,22 +503,10 @@
     image_rows = jnp.transpose(image[:, 0], (1, 0, 2))
     cotan_rows = jnp.transpose(cotangent[:, 0], (1, 0, 2))
     taps = jnp.pad(dw_kernel.reshape(channels, KSIZE * KSIZE), ((0, 0), (0, 128 - KSIZE * KSIZE)))
-    padded = extended(image_rows, "rows").astype(f32)
-    weights = jnp.stack([w_in.T, w_out])
-    weights = jnp.concatenate([weights, swap(weights, "chan", 2)], axis=1)
-    weights = jnp.concatenate([weights, swap(weights, "chan", 1)], axis=1)
-    (mixed_in,) = stencil(
-        forward_kernel, (padded, taps), (jax.ShapeDtypeStruct(image_rows.shape, bf16),)
-    )
     scaled = (layer_scale[:, None] * cotan_rows.astype(f32)).astype(bf16)
     gain_row = jnp.pad(ln_gain[None, None, :], ((0, 0), (0, 0), (0, 128 - channels)))
-    mixed_all, scaled_all, gain_all = exchange(
-        spread_kernel,
-        0,
-        (mixed_in, scaled, gain_row),
-        ((part, n, channels, breadth), (part, n, channels, breadth), (1, n, 1, 128)),
-        n,
-        part,
+    mixed_all, scaled_all, gain_all, weights, padded, mixed_in = lead(
+        n, part, (image_rows, taps, scaled, gain_row, jnp.stack([w_in.T, w_out]))
     )
 
     def flat(value):

time: 135 us -> 124 us (0.919)
  starting transfers between devices: 7.79 us -> 0 us
  waiting for transfers between devices: 5.52 us -> 0 us
  local copies, waits for them, and re-layouts: 9.96 us -> 14.1 us
  other arithmetic: 5.25 us -> 3.53 us
  Pallas kernels: 96.8 us -> 95.1 us
  matrix products: 8.58 us -> 10 us
    ppermute x4 -> x0, starting transfers between devices: 7.79 us -> none  [the longest x1 3.43 us: extended(): low = lax.ppermute(block[-3:], axis, forward)]
    ppermute x4 -> x0, waiting for transfers between devices: 5.52 us -> none  [the longest x2 5.51 us: swap(): return lax.ppermute(value, axis, [(i, i ^ bit) for i in range(n)])]
    pallas_call x1, Pallas kernels: 59.8 us -> 55.8 us  [finish(): pl.pallas_call(functools.partial(finish_kernel, n, rows, part), out_shape...]
    pallas_call x2 -> x1, Pallas kernels: 37.1 us -> 39.3 us  [lead(): pl.pallas_call(functools.partial(lead_kernel, n, rows, part), out_shape=(...]
    unnamed x22 -> x20, local copies, waits for them, and re-layouts: 3.2 us -> 5.26 us
    concatenate x2 -> x0, other arithmetic: 1.51 us -> none  [the longest x1 1.43 us: body(): weights = jnp.concatenate([weights, swap(weights, 'chan', 1)], axis=1)]
    dot_general x1, matrix products: 3.99 us -> 5.41 us  [body(): pre_act = jnp.dot(weights[0], normed, preferred_element_type=f32)]
  transfers between devices with their start and end apart: 4 -> 0, of which waited for: 1 -> 0; matrix products, arithmetic and copies ran while one was open for 5% -> 0% of each run, Pallas kernels for 27% -> 0%
where the time goes in v4:
time: 124 us
  Pallas kernels  95.1 us (77%)
  local copies, waits for them, and re-layouts  14.1 us (11%)
  matrix products  10 us (8%)
  other arithmetic  3.53 us (3%)
    pallas_call x1, Pallas kernels, finish(): pl.pallas_call(functools.partial(finish_kernel, n, rows, part), out_shape...  55.8 us
    pallas_call x1, Pallas kernels, lead(): pl.pallas_call(functools.partial(lead_kernel, n, rows, part), out_shape=(...  39.3 us
    dot_general x1, matrix products, body(): pre_act = jnp.dot(weights[0], normed, preferred_element_type=f32)  5.41 us
    unnamed x20, local copies, waits for them, and re-layouts  5.26 us

profile of v4, /device:TPU:0, one launch (start us, length us, event | category | flops | bytes accessed | tf_op | source)
XLA Modules:
  0.0 123.6 jit_solution(13188839534244325770)
XLA Ops:
  0.6 0.0 copy-start.4
  0.6 0.0 copy-start.5
  0.7 1.2 pad.9.gain_ref
  1.9 0.7 broadcast_in_dim.11.gain_ref
  2.6 0.7 broadcast_in_dim.12.scale_ref
  3.3 0.8 reshape.108
  4.1 0.1 copy.21
  4.2 0.6 pad.8.taps_ref
  4.8 1.7 %copy.31 = bf16[48,1,16,128]{3,0,2,1:T(8,128)(2,1)} copy(bf16[48,1,16,128]{3,2,1,0:T(8,128)(2,1)} %param.7) | data formatting | bytes 393216 | tf_op args[0]
  6.4 1.7 %multiply_convert_fusion.scaled_ref = bf16[16,48,128]{2,1,0:T(8,128)(2,1)} fusion(f32[48]{0:T(128)} %param.12, bf16[48,1,16,128]{3,2,1,0:T(8,128)(2,1)} %param.13), kind=kLoop, calls=%fused_computation.62 | loop fusion | flops 294912 | bytes 393408 | tf_op jit(solution)/shard_map/convert_element_type | solution.py:506
  8.2 1.0 copy.30
  9.2 0.0 copy-done.4
  9.2 0.0 copy-done.5
  9.2 0.9 pad_maximum_fusion.6.weights_ref
  10.0 39.3 %shard_map.126 = (bf16[4,16,48,128]{3,2,1,0:T(8,128)(2,1)}, bf16[4,16,48,128]{3,2,1,0:T(8,128)(2,1)}, f32[1,16,1,128]{3,2,1,0:T(1,128)}, bf16[2,768,768]{2,1,0:T...) custom-call(bf16[16,48,128]{2,1,0:T(8,128)(2,1)} %bitcast.82, f32[48,128]{1,0:T(8,128)} %pad.8.taps_ref, ...), custom_call_target="tpu_custom_call" | custom-call | flops 20000000 | bytes 100000000 | tf_op jit(solution)/shard_map/pallas_call | solution.py:466
  49.3 1.6 %fusion.42 = (bf16[1,16,48,128]{3,2,1,0:T(8,128)(2,1)S(1)}, bf16[1,16,48,128]{3,2,1,0:T(8,128)(2,1)S(1)}, bf16[1,16,48,128]{3,2,1,0:T(8,128)(2,1)S(1)}, bf16[1,1...) fusion(bf16[4,16,48,128]{3,2,1,0:T(8,128)(2,1)} %get-tuple-elem, ...), kind=kLoop, calls=%fused_computation.76 | loop fusion | bytes 3145728 | tf_op jit(solution)/shard_map/slice | solution.py:514
  50.9 0.0 copy-start.6
  50.9 0.2 convert_reduce_fusion
  51.1 0.3 fusion.6
  51.4 0.2 copy-done.6
  51.6 0.1 mul.75
  51.7 0.0 copy-start.7
  51.7 5.4 %fusion.9 = (bf16[768,512]{1,0:T(8,128)(2,1)S(1)}, f32[768,512]{1,0:T(8,128)S(1)}) fusion(f32[768]{0:T(1024)S(1)} %mul.75, f32[512]{0:T(512)S(1)} %add_rsqrt_fusion, f32[512]{0:T(512)S(1)} %broadcast_multiply_fusion, bf16[768,128]{1,0:T(8,128)(2,1)S(1)} %bitcast.100, bf16[768,128]{1,0:T(8,128)(2,1)S(1)} %bitcast.95, bf16[768,128]{1,0:T(8,128)(2,1)S(1)} %bitcast.90, ...), kind=kOutput, calls=%fused_computation.14 | convolution fusion | flops 634257408 | bytes 4332544 | tf_op jit(solution)/shard_map/dot_general | solution.py:528
  57.1 0.0 copy-done.7
  57.1 1.1 fusion.15
  58.3 0.8 convolution_convert_fusion
  59.1 1.0 multiply_reduce_fusion
  60.1 0.1 fusion.43
  60.2 0.1 pad_maximum_fusion.3.branch_ref
  60.3 0.9 fusion.36
  61.2 0.1 fusion.33
  61.3 0.1 slice_bitcast_fusion.1
  61.4 0.8 fusion.35
  62.2 0.1 fusion.34
  62.3 0.1 slice_bitcast_fusion
  62.4 0.2 pad_maximum_fusion.kept_ref
  62.5 0.1 pad_maximum_fusion.1.sent_ref
  62.7 0.0 copy-start
  62.7 0.0 copy-start.1
  62.7 0.0 copy-start.2
  62.7 0.0 copy-start.3
  62.7 0.1 fusion.41
  62.9 0.1 pad_maximum_fusion.5.normed_ref
  63.0 0.6 copy-done
  63.6 0.2 copy-done.1
  63.8 0.0 copy-done.2
  63.8 0.1 copy-done.3
  63.9 55.8 %shard_map.127 = (bf16[16,48,128]{2,1,0:T(8,128)(2,1)S(1)}, bf16[16,48,128]{2,1,0:T(8,128)(2,1)S(1)}, f32[48,128]{1,0:T(8,128)S(1)}, f32[2,192,768]{2,1,0:T(8,128)S(1)}) custom-call(bf16[4,16,48,128]{3,2,1,0:T(8,128)(2,1)S(1)} %pad_maximum_fusion.3.branch_ref, bf16[4,16,48,128]{3,2,1,0:T(8,128)(2,1)S(1)} %pad_maximum_fusion.5.normed_ref, ...), custom_call_target="tpu_custom_call" | custom-call | flops 40000000 | bytes 100000000 | tf_op jit(solution)/shard_map/pallas_call | solution.py:291
  119.7 0.7 copy.24
  120.4 0.7 copy.25
  121.1 0.7 slice_reduce_fusion
  121.8 0.1 copy.23
  121.9 0.6 reshape.109
  122.5 1.1 slice_bitcast_fusion.2
  (4 shorter events, 0.1 us)
Async XLA Ops:
  0.6 8.5 %copy-start.4 = (bf16[192,768]{1,0:T(8,128)(2,1)S(1)}, bf16[192,768]{1,0:T(8,128)(2,1)}, u32[]{:S(2)}) copy-start(bf16[192,768]{1,0:T(8,128)(2,1)} %param.11) | copy-start | bytes 884740
  0.6 8.5 %copy-start.5 = (bf16[768,192]{0,1:T(8,128)(2,1)S(1)}, bf16[768,192]{0,1:T(8,128)(2,1)}, u32[]{:S(2)}) copy-start(bf16[768,192]{0,1:T(8,128)(2,1)} %param.10) | copy-start | bytes 884740
  50.9 0.7 copy-start.6
  51.7 5.4 %copy-start.7 = (bf16[2,768,768]{2,1,0:T(8,128)(2,1)S(1)}, bf16[2,768,768]{2,1,0:T(8,128)(2,1)}, u32[]{:S(2)}) copy-start(bf16[2,768,768]{2,1,0:T(8,128)(2,1)} %get-tuple-element.17) | copy-start | bytes 7077892
  62.7 0.9 copy-start
  62.7 1.1 copy-start.1
  62.7 1.1 copy-start.2
  62.7 1.2 copy-start.3

commit v5 on v4

--- a/solution.py
+++ b/solution.py
@@ -55,8 +55,6 @@
     image_ref,
     cotan_ref,
     taps_ref,
-    gain_ref,
-    scale_ref,
     block_ref,
     image_grad_ref,
     small_ref,
@@ -150,10 +148,24 @@
             ).astype(bf16)
 
     near = pair(1, near_out, near_in, {"chan": flipped(me, 2)})
+    near.wait()
+
+    @pl.loop(0, hidden // 16)
+    def _(i):
+        for a in range(2):
+            own = pl.ds(pl.multiple_of(16 * i, 16), 16)
+            row_out[0, a, own, :] = (grads_ref[a, own, :] + near_in[a, own, :].astype(f32)).astype(
+                bf16
+            )
+
+    step = pair(4, row_out.at[0], row_in.at[0], {"rows": partners[0]})
     for copy in first:
         copy.wait()
     last = scatter(2, lambda peer: branch_ref.at[:, peer], branch_in)
 
+    extra = KSIZE * KSIZE
+    gain = jnp.broadcast_to(taps_ref[:, extra : extra + 1], sums_one.shape)
+    scale = jnp.broadcast_to(taps_ref[:, extra + 1 : extra + 2], sums_one.shape)
     sums_one[...] = jnp.zeros_like(sums_one)
     sums_two[...] = jnp.zeros_like(sums_two)
 
@@ -168,7 +180,7 @@
                 stats += stats_in[p, r]
             unit = (mixed_ref[r].astype(f32) - centre) * inv_scale
             sums_one[...] += grad_normed * unit
-            scaled_grad = grad_normed * gain_ref[...]
+            scaled_grad = grad_normed * gain
             mixed_grad = inv_scale * (
                 scaled_grad - stats[0:1] * (1.0 / D) - unit * (stats[1:2] * (1.0 / D))
             )
@@ -184,17 +196,6 @@
         pair(3, halo_out.at[1], halo_in.at[0], {"rows": down}),
     ]
     normalize(3, height - 3)
-    near.wait()
-
-    @pl.loop(0, hidden // 16)
-    def _(i):
-        for a in range(2):
-            own = pl.ds(pl.multiple_of(16 * i, 16), 16)
-            row_out[0, a, own, :] = (grads_ref[a, own, :] + near_in[a, own, :].astype(f32)).astype(
-                bf16
-            )
-
-    step = pair(4, row_out.at[0], row_in.at[0], {"rows": partners[0]})
     for copy in halos:
         copy.wait()
     above = jnp.where(row > 0, 1.0, 0.0).astype(f32)
@@ -261,7 +262,7 @@
         for p in range(1, planes):
             branch += branch_in[p, r].astype(f32)
         sums_two[...] += branch * cotan_ref[r].astype(f32)
-        block_ref[r] = (image_ref[r].astype(f32) + scale_ref[...] * branch).astype(bf16)
+        block_ref[r] = (image_ref[r].astype(f32) + scale * branch).astype(bf16)
 
     lane = lax.broadcasted_iota(jnp.int32, small_ref.shape, 1)
     small = small_ref[...]
@@ -296,7 +297,7 @@
             jax.ShapeDtypeStruct((channels, 128), f32),
             jax.ShapeDtypeStruct((2, hidden, width), f32),
         ),
-        in_specs=[hbm] * 4 + [vmem] * 8,
+        in_specs=[hbm] * 4 + [vmem] * 6,
         out_specs=(vmem, vmem, vmem, vmem),
         scratch_shapes=[
             pltpu.VMEM((planes, height, channels, breadth), bf16),
@@ -502,7 +503,15 @@
     bf16, f32 = jnp.bfloat16, jnp.float32
     image_rows = jnp.transpose(image[:, 0], (1, 0, 2))
     cotan_rows = jnp.transpose(cotangent[:, 0], (1, 0, 2))
-    taps = jnp.pad(dw_kernel.reshape(channels, KSIZE * KSIZE), ((0, 0), (0, 128 - KSIZE * KSIZE)))
+    taps = jnp.concatenate(
+        [
+            dw_kernel.reshape(channels, KSIZE * KSIZE),
+            ln_gain[:, None],
+            layer_scale[:, None],
+            jnp.zeros((channels, 126 - KSIZE * KSIZE), f32),
+        ],
+        axis=1,
+    )
     scaled = (layer_scale[:, None] * cotan_rows.astype(f32)).astype(bf16)
     gain_row = jnp.pad(ln_gain[None, None, :], ((0, 0), (0, 0), (0, 128 - channels)))
     mixed_all, scaled_all, gain_all, weights, padded, mixed_in = lead(
@@ -557,8 +566,6 @@
             image_rows,
             cotan_rows,
             taps,
-            jnp.broadcast_to(ln_gain[:, None], (channels, breadth)),
-            jnp.broadcast_to(layer_scale[:, None], (channels, breadth)),
         ),
         half // 2,
     )

time: 124 us -> 128 us (1.032)
  Pallas kernels: 95.1 us -> 98.9 us
    pallas_call x1, Pallas kernels: 55.8 us -> 59.7 us  [finish(): pl.pallas_call(functools.partial(finish_kernel, n, rows, part), out_shape...]
where the time goes in v5:
time: 128 us
  Pallas kernels  98.9 us (77%)
  local copies, waits for them, and re-layouts  13.6 us (11%)
  matrix products  10 us (8%)
  other arithmetic  4.23 us (3%)
    pallas_call x1, Pallas kernels, finish(): pl.pallas_call(functools.partial(finish_kernel, n, rows, part), out_shape...  59.7 us
    pallas_call x1, Pallas kernels, lead(): pl.pallas_call(functools.partial(lead_kernel, n, rows, part), out_shape=(...  39.3 us
    dot_general x1, matrix products, body(): pre_act = jnp.dot(weights[0], normed, preferred_element_type=f32)  5.41 us
    unnamed x20, local copies, waits for them, and re-layouts  5.26 us

profile of v5, /device:TPU:0, one launch (start us, length us, event | category | flops | bytes accessed | tf_op | source)
XLA Modules:
  0.0 127.7 jit_solution(15387141812453513161)
XLA Ops:
  0.6 0.0 copy-start.4
  0.6 0.0 copy-start.5
  0.7 1.2 pad.4.gain_ref
  1.9 0.1 pad.34.clone
  2.0 0.7 copy.25
  2.7 0.7 copy.24
  3.4 0.8 reshape.106
  4.2 0.1 copy.23
  4.3 0.7 maximum_maximum_fusion.taps_ref
  5.0 1.7 %copy.35 = bf16[48,1,16,128]{3,0,2,1:T(8,128)(2,1)} copy(bf16[48,1,16,128]{3,2,1,0:T(8,128)(2,1)} %param.7) | data formatting | bytes 393216 | tf_op args[0]
  6.6 1.7 %multiply_convert_fusion.scaled_ref = bf16[16,48,128]{2,1,0:T(8,128)(2,1)} fusion(f32[48]{0:T(128)} %param.12, bf16[48,1,16,128]{3,2,1,0:T(8,128)(2,1)} %param.13), kind=kLoop, calls=%fused_computation.62 | loop fusion | flops 294912 | bytes 393408 | tf_op jit(solution)/shard_map/convert_element_type | solution.py:515
  8.4 1.0 copy.34
  9.3 0.0 copy-done.4
  9.3 0.0 copy-done.5
  9.4 0.9 pad_maximum_fusion.6.weights_ref
  10.2 39.3 %shard_map.126 = (bf16[4,16,48,128]{3,2,1,0:T(8,128)(2,1)}, bf16[4,16,48,128]{3,2,1,0:T(8,128)(2,1)}, f32[1,16,1,128]{3,2,1,0:T(1,128)}, bf16[2,768,768]{2,1,0:T...) custom-call(bf16[16,48,128]{2,1,0:T(8,128)(2,1)} %bitcast.84, ...), custom_call_target="tpu_custom_call" | custom-call | flops 20000000 | bytes 100000000 | tf_op jit(solution)/shard_map/pallas_call | solution.py:467
  49.5 1.6 %fusion.42 = (bf16[1,16,48,128]{3,2,1,0:T(8,128)(2,1)S(1)}, bf16[1,16,48,128]{3,2,1,0:T(8,128)(2,1)S(1)}, bf16[1,16,48,128]{3,2,1,0:T(8,128)(2,1)S(1)}, bf16[1,1...) fusion(bf16[4,16,48,128]{3,2,1,0:T(8,128)(2,1)} %get-tuple-elem, ...), kind=kLoop, calls=%fused_computation.77 | loop fusion | bytes 3145728 | tf_op jit(solution)/shard_map/slice | solution.py:523
  51.1 0.0 copy-start.6
  51.1 0.2 convert_reduce_fusion
  51.3 0.3 fusion.6
  51.6 0.2 copy-done.6
  51.8 0.1 mul.75
  51.9 0.0 copy-start.7
  51.9 5.4 %fusion.9 = (bf16[768,512]{1,0:T(8,128)(2,1)S(1)}, f32[768,512]{1,0:T(8,128)S(1)}) fusion(f32[768]{0:T(1024)S(1)} %mul.75, f32[512]{0:T(512)S(1)} %add_rsqrt_fusion, f32[512]{0:T(512)S(1)} %broadcast_multiply_fusion, bf16[768,128]{1,0:T(8,128)(2,1)S(1)} %bitcast.102, bf16[768,128]{1,0:T(8,128)(2,1)S(1)} %bitcast.97, bf16[768,128]{1,0:T(8,128)(2,1)S(1)} %bitcast.92, ...), kind=kOutput, calls=%fused_computation.14 | convolution fusion | flops 634257408 | bytes 4332544 | tf_op jit(solution)/shard_map/dot_general | solution.py:537
  57.3 0.0 copy-done.7
  57.3 1.1 fusion.15
  58.5 0.8 convolution_convert_fusion
  59.3 1.0 multiply_reduce_fusion
  60.2 0.1 fusion.43
  60.4 0.1 pad_maximum_fusion.3.branch_ref
  60.5 0.9 fusion.36
  61.4 0.1 fusion.33
  61.5 0.1 slice_bitcast_fusion.1
  61.6 0.8 fusion.35
  62.4 0.1 fusion.34
  62.5 0.1 slice_bitcast_fusion
  62.6 0.2 pad_maximum_fusion.kept_ref
  62.7 0.1 pad_maximum_fusion.1.sent_ref
  62.9 0.0 copy-start
  62.9 0.0 copy-start.1
  62.9 0.0 copy-start.2
  62.9 0.0 copy-start.3
  62.9 0.1 fusion.41
  63.0 0.1 pad_maximum_fusion.5.normed_ref
  63.2 0.6 copy-done
  63.8 0.2 copy-done.1
  64.0 0.0 copy-done.2
  64.0 0.1 copy-done.3
  64.1 59.7 %shard_map.127 = (bf16[16,48,128]{2,1,0:T(8,128)(2,1)S(1)}, bf16[16,48,128]{2,1,0:T(8,128)(2,1)S(1)}, f32[48,128]{1,0:T(8,128)S(1)}, f32[2,192,768]{2,1,0:T(8,128)S(1)}) custom-call(bf16[4,16,48,128]{3,2,1,0:T(8,128)(2,1)S(1)} %pad_maximum_fusion.3.branch_ref, bf16[4,16,48,128]{3,2,1,0:T(8,128)(2,1)S(1)} %pad_maximum_fusion.5.normed_ref, ...), custom_call_target="tpu_custom_call" | custom-call | flops 40000000 | bytes 100000000 | tf_op jit(solution)/shard_map/pallas_call | solution.py:292
  123.7 0.7 copy.28
  124.5 0.7 copy.29
  125.2 0.7 slice_reduce_fusion
  125.9 0.1 copy.27
  126.0 0.6 reshape.107
  126.6 1.1 slice_bitcast_fusion.2
  (5 shorter events, 0.1 us)
Async XLA Ops:
  0.6 8.7 %copy-start.4 = (bf16[192,768]{1,0:T(8,128)(2,1)S(1)}, bf16[192,768]{1,0:T(8,128)(2,1)}, u32[]{:S(2)}) copy-start(bf16[192,768]{1,0:T(8,128)(2,1)} %param.11) | copy-start | bytes 884740
  0.6 8.7 %copy-start.5 = (bf16[768,192]{0,1:T(8,128)(2,1)S(1)}, bf16[768,192]{0,1:T(8,128)(2,1)}, u32[]{:S(2)}) copy-start(bf16[768,192]{0,1:T(8,128)(2,1)} %param.10) | copy-start | bytes 884740
  51.1 0.7 copy-start.6
  51.9 5.4 %copy-start.7 = (bf16[2,768,768]{2,1,0:T(8,128)(2,1)S(1)}, bf16[2,768,768]{2,1,0:T(8,128)(2,1)}, u32[]{:S(2)}) copy-start(bf16[2,768,768]{2,1,0:T(8,128)(2,1)} %get-tuple-element.17) | copy-start | bytes 7077892
  62.9 0.9 copy-start
  62.9 1.1 copy-start.1
  62.9 1.1 copy-start.2
  62.9 1.2 copy-start.3
